TPU v7x, 512 devices: a whole 4x8x8 slice. The times are simulated.
512 devices in a mesh: lat: 32 (over z_hi, y), lon: 16 (over z_lo, x, core).
Axes of the slice: x: 4, y: 8, z: 8 (z_hi: 4, z_lo: 2; z = z_hi * 2 + z_lo), core: 2. Of those that a mesh axis runs over, the one named last changes fastest.
Arguments:
- obs_values: float32 [16, 2097152], P(None, ('lat', 'lon')), may hold values from -6 to 6
- obs_rows: int32 [2097152], P(('lat', 'lon')), may hold values from 0 to 95
- obs_cols: int32 [2097152], P(('lat', 'lon')), may hold values from 0 to 383
- row_frac: float32 [2097152], P(('lat', 'lon')), may hold values from 0 to 1
- col_frac: float32 [2097152], P(('lat', 'lon')), may hold values from 0 to 1
- obs_count: int32 [512], P(('lat', 'lon')), may hold values from 1 to 4096, 1572864 in all
- sigma: float32 [3072, 16, 6144], P('lat', None, 'lon'), may hold values from 0.3 to 3
- lat_scales: float32 [16], replicated, may hold values from 40 to 64
- lon_scales: float32 [16], replicated, may hold values from 40 to 64
Outputs:
- control: float32 [3072, 16, 6144], P('lat', None, 'lon')
Inputs may be any that keep to these rules, and one draw needn't show every extreme that they name: Tile d (latitude tile d // 16, longitude tile d % 16) holds slots d * 4096 to (d + 1) * 4096 - 1, of which the first obs_count[d] are live; some tile has all 4096 live. `obs_rows`: counted within the observation's own tile. `obs_cols`: counted within the observation's own tile.
All inputs are finite; a program needn't handle non-finite values. No bound on the sum of `obs_count` on one device may be relied on, other than what follows from the above.
Results may differ from a plain program's by a relative error of at most 0.000098.
Values sent between devices are 32-bit elements; how exact they have to be, the bound alone decides.
A program may use at most 128 MiB of HBM per device.

v0:
```python
import jax
import jax.numpy as jnp
from jax import lax
from jax.sharding import PartitionSpec as P

HALF = 128


def from_behind(block, axis, distance):
    devices = range(lax.axis_size(axis))
    route = [((i - distance) % len(devices), i) for i in devices]
    return lax.ppermute(block, axis, route)


def shifted(block, axis, distance):
    devices = range(lax.axis_size(axis))
    route = [(i - distance, i) for i in devices if i - distance in devices]
    return lax.ppermute(block, axis, route)


def with_halo(block, sides, width):
    for axis, dim in sides:
        count = lax.axis_size(axis)
        forward = [(i, i + 1) for i in range(count - 1)]
        forward.append((count - 1, 0))
        backward = [(target, source) for source, target in forward]
        low = lax.ppermute(
            lax.slice_in_dim(block, block.shape[dim] - width, None, axis=dim), axis, forward
        )
        high = lax.ppermute(lax.slice_in_dim(block, 0, width, axis=dim), axis, backward)
        block = jnp.concatenate([low, block, high], axis=dim)
    return block


def kernel_matrix(scales, out_count, half_width):
    out_index = jnp.arange(out_count, dtype=jnp.int32)[:, None]
    in_index = jnp.arange(out_count + 2 * half_width, dtype=jnp.int32)[None, :]
    offset = in_index - half_width - out_index
    inside = jnp.abs(offset) <= half_width
    offset_real = offset.astype(jnp.float32)
    spread = scales[:, None, None]
    tap_lag = jnp.arange(-half_width, half_width + 1, dtype=jnp.int32).astype(jnp.float32)
    energy = jnp.sum(
        jnp.exp(-(tap_lag[None, :] * tap_lag[None, :]) / (spread[:, :, 0] * spread[:, :, 0])),
        axis=1,
    )
    gaussian = (
        jnp.exp(-(offset_real * offset_real)[None] / (2.0 * spread * spread))
        / jnp.sqrt(energy)[:, None, None]
    )
    return jnp.where(inside[None], gaussian, jnp.zeros_like(gaussian))


def corner_weights(index, frac, count):
    cells = jnp.arange(count, dtype=jnp.int32)[None, :]
    low = jnp.where(cells == index[:, None], (1.0 - frac)[:, None], 0.0)
    high = jnp.where(cells == index[:, None] + 1, frac[:, None], 0.0)
    return low + high


def lat_halo(block, width):
    rows = block.shape[0]
    parts = []
    reach = width
    distance = 1
    below, above = [], []
    while reach > 0:
        take = min(rows, reach)
        below.insert(0, shifted(block[rows - take :], "lat", distance))
        above.append(shifted(block[:take], "lat", -distance))
        reach -= take
        distance += 1
    parts = below + [block] + above
    return jnp.concatenate(parts, axis=0)


def shards(
    obs_values, obs_rows, obs_cols, row_frac, col_frac, obs_count, sigma, lat_scales, lon_scales
):
    tile_rows, level_count, tile_cols = sigma.shape
    slot_total = obs_rows.shape[0]
    live_slot = jnp.arange(slot_total, dtype=jnp.int32) < obs_count[0]
    values_t = jnp.where(live_slot[:, None], jnp.transpose(obs_values), 0.0)
    row_w = corner_weights(obs_rows, row_frac, tile_rows + 1)
    col_w = corner_weights(obs_cols, col_frac, tile_cols + 1)
    row_values = row_w[:, :, None] * values_t[:, None, :]
    extended = jnp.einsum(
        "krl,kc->rlc", row_values, col_w, precision=lax.Precision.HIGH
    )
    edge_column = from_behind(extended[:, :, tile_cols], "lon", 1)
    folded = jnp.concatenate(
        [(extended[:, :, 0] + edge_column)[:, :, None], extended[:, :, 1:tile_cols]], axis=2
    )
    edge_row = shifted(folded[tile_rows], "lat", 1)
    departures = jnp.concatenate([(folded[0] + edge_row)[None], folded[1:tile_rows]], axis=0)
    weighted = departures * sigma
    half_width = HALF
    window = lat_halo(weighted, half_width)
    lat_kernel = kernel_matrix(lat_scales, tile_rows, half_width)
    lat_done = jnp.einsum(
        "lip,plc->ilc", lat_kernel, window, precision=lax.Precision.HIGH
    )
    padded_cols = with_halo(lat_done, (("lon", 2),), half_width)
    band = half_width
    lon_kernel = kernel_matrix(lon_scales, band, half_width)
    band_count = tile_cols // band
    bands = jnp.stack(
        [padded_cols[:, :, b * band : b * band + band + 2 * half_width] for b in range(band_count)],
        axis=2,
    )
    result = jnp.einsum("lip,rlbp->rlbi", lon_kernel, bands, precision=lax.Precision.HIGH)
    return result.reshape(tile_rows, level_count, tile_cols)


def solution(mesh):
    in_specs = (
        P(None, ("lat", "lon")),
        P(("lat", "lon")),
        P(("lat", "lon")),
        P(("lat", "lon")),
        P(("lat", "lon")),
        P(("lat", "lon")),
        P("lat", None, "lon"),
        P(),
        P(),
    )
    out_specs = P("lat", None, "lon")
    return jax.shard_map(shards, mesh=mesh, in_specs=in_specs, out_specs=out_specs, check_vma=False)
```

profile of v0, /device:TPU:113, one launch (start us, length us, event | category | flops | bytes accessed | tf_op | source)
XLA Modules:
  0.0 267.9 jit_solution(13773015742722594924)
XLA Ops:
  0.0 0.7 broadcast_add_fusion
  0.7 0.7 broadcast_subtract_fusion
  1.4 0.7 broadcast_add_fusion.1
  2.2 0.7 broadcast_subtract_fusion.1
  3.5 0.0 copy-start.4
  3.6 0.0 copy-start.5
  3.6 0.0 copy-start.3
  3.6 4.5 %fusion.60 = f32[4096,385,1]{0,1,2:T(8,128)} fusion(f32[4096]{0:T(1024)} %param.13, s32[4096]{0:T(1024)S(1)} %broadcast_add_fusion, f32[4096]{0:T(1024)S(1)} %broadcast_subtract_fusion, s32[4096]{0:T(1024)} %param.11), kind=kLoop, calls=%fused_computation.9.clone.2 | loop fusion | flops 7884800 | bytes 6373376 | tf_op jit(solution)/shard_map/krl,kc->rlc/dot_general | solution.py:87
  8.1 0.0 copy-done.4
  8.1 0.0 copy-done.5
  8.1 1.5 select_add_fusion
  9.6 0.0 copy-done.3
  9.6 29.1 %fusion = f32[97,16,385]{2,1,0:T(8,128)S(1)} fusion(f32[4096,16]{0,1:T(8,128)S(1)} %select_bitcast_fusion, f32[4096,97]{0,1:T(8,128)} %select_add_fusion, f32[4096,385,1]{0,1,2:T(8,128)} %fusion.60), kind=kOutput, calls=%fused_computation | convolution fusion | flops 14691008512 | bytes 10549312 | tf_op jit(solution)/shard_map/krl,kc->rlc/dot_general | solution.py:87
  38.7 0.0 copy-start
  38.7 1.4 fusion.51
  40.1 1.7 copy.34
  41.7 0.0 copy-done
  41.8 3.7 %collective-permute-start = (f32[97,16]{0,1:T(8,128)S(1)}, f32[97,16]{0,1:T(8,128)S(1)}, u32[]{:S(2)}, u32[]{:S(2)}) collective-permute-start(f32[97,16]{0,1:T(8,128)S(1)} %bitcast.48), channel_id=1, source_target_pairs={{15,0},{0,1},{1,2},{2,3},{3,4},{4,5},{5,6},{6,7},{7,8},{8,9},{9,10... | collective-permute-start | bytes 18632 | tf_op jit(solution)/shard_map/ppermute | solution.py:12
  45.4 0.0 copy-start.1
  45.4 2.6 slice.52
  48.1 0.0 copy-done.1
  48.1 0.4 copy.33
  48.5 0.0 collective-permute-done
  48.5 0.5 copy.35
  48.9 0.1 maximum_bitcast_fusion
  49.0 0.0 copy-start.2
  49.0 2.4 collective-permute-start.1
  51.5 2.3 collective-permute-done.1
  53.7 0.1 fusion.46
  53.8 0.0 copy-done.2
  53.8 0.0 copy-start.6
  53.8 0.0 copy-start.7
  53.8 0.7 fusion.27
  54.5 3.7 %collective-permute-start.3 = (f32[96,16,384]{2,1,0:T(8,128)S(1)}, f32[96,16,384]{2,1,0:T(8,128)S(1)}, u32[]{:S(2)}, u32[]{:S(2)}) collective-permute-start(f32[96,16,384]{2,1,0:T(8,128)S(1)} %fusion.27), channel_id=1, source_target_pairs={{0,16},{16,32},{32,48},{48,64},{64,80},{80,96},{96,112},{112,128},... | collective-permute-start | bytes 7077896 | tf_op jit(solution)/shard_map/ppermute | solution.py:18
  58.2 1.9 collective-permute-start.4
  60.1 0.0 copy-done.6
  60.2 0.0 copy-done.7
  60.2 0.1 fusion.53
  60.3 10.8 %collective-permute-start.2 = (f32[32,16,384]{2,1,0:T(8,128)S(1)}, f32[32,16,384]{2,1,0:T(8,128)S(1)}, u32[]{:S(2)}, u32[]{:S(2)}) collective-permute-start(f32[32,16,384]{2,1,0:T(8,128)S(1)} %get-tuple-element.14), channel_id=1, source_target_pairs={{0,32},{16,48},{32,64},{48,80},{64,96},{80,112},{96,128},{112,144}... | collective-permute-start | bytes 2359304 | tf_op jit(solution)/shard_map/ppermute | solution.py:18
  71.2 0.2 fusion.44
  71.4 1.9 collective-permute-start.5
  73.4 76.6 %collective-permute-done.2 = f32[32,16,384]{2,1,0:T(8,128)S(1)} collective-permute-done((f32[32,16,384]{2,1,0:T(8,128)S(1)}, f32[32,16,384]{2,1,0:T(8,128)S(1)}, u32[]{:S(2)}, u32[]{:S(2)}) %collective-permute-start.2) | collective-permute-done | bytes 786464 | tf_op jit(solution)/shard_map/ppermute | solution.py:18
  150.0 0.1 constant_dynamic-update-slice_fusion.4
  150.1 0.0 collective-permute-done.3
  150.1 0.2 constant_dynamic-update-slice_fusion.3
  150.3 0.2 constant_dynamic-update-slice_fusion.2
  150.4 0.0 collective-permute-done.4
  150.4 0.2 constant_dynamic-update-slice_fusion.1
  150.6 76.5 %collective-permute-done.5 = f32[32,16,384]{2,1,0:T(8,128)S(1)} collective-permute-done((f32[32,16,384]{2,1,0:T(8,128)S(1)}, f32[32,16,384]{2,1,0:T(8,128)S(1)}, u32[]{:S(2)}, u32[]{:S(2)}) %collective-permute-start.5) | collective-permute-done | bytes 786464 | tf_op jit(solution)/shard_map/ppermute | solution.py:18
  227.1 0.1 constant_dynamic-update-slice_fusion
  227.2 5.8 %fusion.4 = f32[16,384,96]{1,2,0:T(8,128)S(1)} fusion(f32[352,16,384]{2,1,0:T(8,128)S(1)} %constant_dynamic-update-slice_fusion, f32[16]{0:T(128)S(1)} %sqrt.14, f32[16]{0:T(128)S(1)} %get-tuple-element.17, f32[96,352]{1,0:T(8,128)S(1)} %multiply_negate_fusion.1, pred[96,352]{1,0:T(8,128)(4,1)S(1)} %abs_compare_fusion.1), kind=kOutput, calls=%fused_computation.4 | convolution fusion | flops 1247330304 | bytes 11179136 | tf_op jit(solution)/shard_map/lip,plc->ilc/dot_general | solution.py:100
  233.0 0.2 fusion.52
  233.1 13.4 %collective-permute-start.6 = (f32[96,16,128]{2,0,1:T(8,128)S(1)}, f32[96,16,128]{2,0,1:T(8,128)S(1)}, u32[]{:S(2)}, u32[]{:S(2)}) collective-permute-start(f32[96,16,128]{2,0,1:T(8,128)S(1)} %get-tuple-element.11), channel_id=1, source_target_pairs={{0,1},{1,2},{2,3},{3,4},{4,5},{5,6},{6,7},{7,8},{8,9},{9,10},{10,1... | collective-permute-start | bytes 2359304 | tf_op jit(solution)/shard_map/ppermute | solution.py:27
  246.5 2.1 collective-permute-start.7
  248.7 0.1 abs_compare_fusion
  248.8 6.6 %collective-permute-done.6 = f32[96,16,128]{2,0,1:T(8,128)S(1)} collective-permute-done((f32[96,16,128]{2,0,1:T(8,128)S(1)}, f32[96,16,128]{2,0,1:T(8,128)S(1)}, u32[]{:S(2)}, u32[]{:S(2)}) %collective-permute-start.6) | collective-permute-done | bytes 786464 | tf_op jit(solution)/shard_map/ppermute | solution.py:27
  255.4 4.4 %collective-permute-done.7 = f32[96,16,128]{2,0,1:T(8,128)S(1)} collective-permute-done((f32[96,16,128]{2,0,1:T(8,128)S(1)}, f32[96,16,128]{2,0,1:T(8,128)S(1)}, u32[]{:S(2)}, u32[]{:S(2)}) %collective-permute-start.7) | collective-permute-done | bytes 786464 | tf_op jit(solution)/shard_map/ppermute | solution.py:30
  259.8 0.4 fusion.25
  260.2 3.5 %fusion.28 = f32[96,16,3,128]{3,0,2,1:T(8,128)S(1)} fusion(f32[16]{0:T(128)S(1)} %sqrt.15, f32[16]{0:T(128)S(1)} %get-tuple-element.15, f32[128,384]{1,0:T(8,128)S(1)} %multiply_negate_fusion, pred[128,384]{1,0:T(8,128)(4,1)S(1)} %abs_compare_fusion, f32[96,16,1,384]{3,0,1,2:T(8,128)S(1)} %get-tuple-element.10, f32[96,16,1,384]{3,0,1,2:T(8,128)S(1)} %bitcast.47, ...), kind=kOutput, calls=%fused_computation.38 | convolution fusion | flops 1364852736 | bytes 9683072 | tf_op jit(solution)/shard_map/lip,rlbp->rlbi/dot_general | solution.py:111
  263.7 1.6 copy.38
  265.3 2.6 reshape.212
  (13 shorter events, 0.2 us)
Async XLA Ops:
  3.5 4.6 %copy-start.4 = (f32[4096]{0:T(1024)S(1)}, f32[4096]{0:T(1024)}, u32[]{:S(2)}) copy-start(f32[4096]{0:T(1024)} %param.12) | copy-start | bytes 49156
  3.6 4.5 %copy-start.5 = (s32[4096]{0:T(1024)S(1)}, s32[4096]{0:T(1024)}, u32[]{:S(2)}) copy-start(s32[4096]{0:T(1024)} %param.10) | copy-start | bytes 49156
  3.6 6.0 %copy-start.3 = (f32[16,4096]{1,0:T(8,128)S(1)}, f32[16,4096]{1,0:T(8,128)}, u32[]{:S(2)}) copy-start(f32[16,4096]{1,0:T(8,128)} %param.9) | copy-start | bytes 786436
  38.7 3.1 %copy-start = (f32[97,16,385]{2,1,0:T(8,128)}, f32[97,16,385]{2,1,0:T(8,128)S(1)}, u32[]{:S(2)}) copy-start(f32[97,16,385]{2,1,0:T(8,128)S(1)} %fusion) | copy-start | bytes 7170244
  41.8 6.7 %collective-permute-start = (f32[97,16]{0,1:T(8,128)S(1)}, f32[97,16]{0,1:T(8,128)S(1)}, u32[]{:S(2)}, u32[]{:S(2)}) collective-permute-start(f32[97,16]{0,1:T(8,128)S(1)} %bitcast.48), channel_id=1, source_target_pairs={{15,0},{0,1},{1,2},{2,3},{3,4},{4,5},{5,6},{6,7},{7,8},{8,9},{9,10... | collective-permute-start | bytes 18632 | tf_op jit(solution)/shard_map/ppermute | solution.py:12
  45.4 2.7 copy-start.1
  49.0 4.8 %copy-start.2 = (f32[96,16,384]{2,1,0:T(8,128)S(1)}, f32[96,16,384]{2,1,0:T(8,128)}, u32[]{:S(2)}) copy-start(f32[96,16,384]{2,1,0:T(8,128)} %param.15) | copy-start | bytes 7077892
  49.0 4.7 %collective-permute-start.1 = (f32[16,384]{1,0:T(8,128)S(1)}, f32[16,384]{1,0:T(8,128)S(1)}, u32[]{:S(2)}, u32[]{:S(2)}) collective-permute-start(f32[16,384]{1,0:T(8,128)S(1)} %maximum_bitcast_fusion), channel_id=1, source_target_pairs={{0,16},{16,32},{32,48},{48,64},{64,80},{80,96},{96,112},{112,128},... | collective-permute-start | bytes 73736 | tf_op jit(solution)/shard_map/ppermute | solution.py:18
  53.8 6.4 %copy-start.6 = (f32[16]{0:T(128)S(1)}, f32[16]{0:T(128)}, u32[]{:S(2)}) copy-start(f32[16]{0:T(128)} %param.17) | copy-start | bytes 196
  53.8 6.4 %copy-start.7 = (f32[16]{0:T(128)S(1)}, f32[16]{0:T(128)}, u32[]{:S(2)}) copy-start(f32[16]{0:T(128)} %param.16) | copy-start | bytes 196
  54.5 95.6 %collective-permute-start.3 = (f32[96,16,384]{2,1,0:T(8,128)S(1)}, f32[96,16,384]{2,1,0:T(8,128)S(1)}, u32[]{:S(2)}, u32[]{:S(2)}) collective-permute-start(f32[96,16,384]{2,1,0:T(8,128)S(1)} %fusion.27), channel_id=1, source_target_pairs={{0,16},{16,32},{32,48},{48,64},{64,80},{80,96},{96,112},{112,128},... | collective-permute-start | bytes 7077896 | tf_op jit(solution)/shard_map/ppermute | solution.py:18
  58.2 92.2 %collective-permute-start.4 = (f32[96,16,384]{2,1,0:T(8,128)S(1)}, f32[96,16,384]{2,1,0:T(8,128)S(1)}, u32[]{:S(2)}, u32[]{:S(2)}) collective-permute-start(f32[96,16,384]{2,1,0:T(8,128)S(1)} %fusion.27), channel_id=1, source_target_pairs={{16,0},{32,16},{48,32},{64,48},{80,64},{96,80},{112,96},{128,112},... | collective-permute-start | bytes 7077896 | tf_op jit(solution)/shard_map/ppermute | solution.py:18
  60.3 89.7 %collective-permute-start.2 = (f32[32,16,384]{2,1,0:T(8,128)S(1)}, f32[32,16,384]{2,1,0:T(8,128)S(1)}, u32[]{:S(2)}, u32[]{:S(2)}) collective-permute-start(f32[32,16,384]{2,1,0:T(8,128)S(1)} %get-tuple-element.14), channel_id=1, source_target_pairs={{0,32},{16,48},{32,64},{48,80},{64,96},{80,112},{96,128},{112,144}... | collective-permute-start | bytes 2359304 | tf_op jit(solution)/shard_map/ppermute | solution.py:18
  71.4 155.7 %collective-permute-start.5 = (f32[32,16,384]{2,1,0:T(8,128)S(1)}, f32[32,16,384]{2,1,0:T(8,128)S(1)}, u32[]{:S(2)}, u32[]{:S(2)}) collective-permute-start(f32[32,16,384]{2,1,0:T(8,128)S(1)} %get-tuple-element.13), channel_id=1, source_target_pairs={{32,0},{48,16},{64,32},{80,48},{96,64},{112,80},{128,96},{144,112}... | collective-permute-start | bytes 2359304 | tf_op jit(solution)/shard_map/ppermute | solution.py:18
  233.1 22.3 %collective-permute-start.6 = (f32[96,16,128]{2,0,1:T(8,128)S(1)}, f32[96,16,128]{2,0,1:T(8,128)S(1)}, u32[]{:S(2)}, u32[]{:S(2)}) collective-permute-start(f32[96,16,128]{2,0,1:T(8,128)S(1)} %get-tuple-element.11), channel_id=1, source_target_pairs={{0,1},{1,2},{2,3},{3,4},{4,5},{5,6},{6,7},{7,8},{8,9},{9,10},{10,1... | collective-permute-start | bytes 2359304 | tf_op jit(solution)/shard_map/ppermute | solution.py:27
  246.5 13.3 %collective-permute-start.7 = (f32[96,16,128]{2,0,1:T(8,128)S(1)}, f32[96,16,128]{2,0,1:T(8,128)S(1)}, u32[]{:S(2)}, u32[]{:S(2)}) collective-permute-start(f32[96,16,128]{2,0,1:T(8,128)S(1)} %get-tuple-element.12), channel_id=1, source_target_pairs={{1,0},{2,1},{3,2},{4,3},{5,4},{6,5},{7,6},{8,7},{9,8},{10,9},{11,1... | collective-permute-start | bytes 2359304 | tf_op jit(solution)/shard_map/ppermute | solution.py:30
where the time goes:
time: 269 us; the launch traced here: 268 us
  waiting for transfers between devices  166 us (62%)
  starting transfers between devices  39.9 us (15%)
  matrix products  38.3 us (14%)
  local copies, waits for them, and re-layouts  11.7 us (4%)
  other arithmetic  10.5 us (4%)
    ppermute x5, waiting for transfers between devices, shifted(): return lax.ppermute(block, axis, route)  155 us
    dot_general x1, matrix products, shards(): jnp.einsum('krl,kc->rlc', row_values, col_w, precision=lax.Precision.HIGH)  29.1 us
    ppermute x5, starting transfers between devices, shifted(): return lax.ppermute(block, axis, route)  20.8 us
    ppermute x1, starting transfers between devices, with_halo(): lax.ppermute(lax.slice_in_dim(block, block.shape[dim] - width, None, axis...  13.4 us
    ppermute x1, waiting for transfers between devices, with_halo(): lax.ppermute(lax.slice_in_dim(block, block.shape[dim] - width, None, axis...  6.63 us
    dot_general x1, matrix products, shards(): jnp.einsum('lip,plc->ilc', lat_kernel, window, precision=lax.Precision.HIGH)  5.79 us
  transfers between devices with their start and end apart: 8, of which 5 were waited for; matrix products, arithmetic and copies ran while one was open for 2% of the time, Pallas kernels for 0%

commit v1 on v0

--- a/solution.py
+++ b/solution.py
@@ -1,6 +1,10 @@
+import functools
+
 import jax
 import jax.numpy as jnp
 from jax import lax
+from jax.experimental import pallas as pl
+from jax.experimental.pallas import tpu as pltpu
 from jax.sharding import PartitionSpec as P
 
 HALF = 128
@@ -74,6 +78,64 @@
     return jnp.concatenate(parts, axis=0)
 
 
+def halo_body(count, rows, far, x_ref, below_ref, above_ref, send_sem, recv_sem):
+    here = lax.axis_index("lat")
+    column = lax.axis_index("lon")
+    mesh = pl.DeviceIdType.MESH
+    barrier = pltpu.get_barrier_semaphore()
+    partners = ((1, 0), (2, 1), (-1, 2), (-2, 3))
+    for step, slot in partners:
+        neighbour = lax.rem(here + step + count, count)
+        pl.semaphore_signal(barrier, 1, device_id=(neighbour, column), device_id_type=mesh)
+    pl.semaphore_wait(barrier, len(partners))
+
+    def copy(step, slot, device):
+        if step == 1:
+            src, dst = x_ref, below_ref.at[pl.ds(far, rows)]
+        elif step == 2:
+            src, dst = x_ref.at[pl.ds(rows - far, far)], below_ref.at[pl.ds(0, far)]
+        elif step == -1:
+            src, dst = x_ref, above_ref.at[pl.ds(0, rows)]
+        else:
+            src, dst = x_ref.at[pl.ds(0, far)], above_ref.at[pl.ds(rows, far)]
+        return pltpu.make_async_remote_copy(
+            src_ref=src, dst_ref=dst, send_sem=send_sem.at[slot], recv_sem=recv_sem.at[slot],
+            device_id=(device, column), device_id_type=mesh,
+        )
+
+    for step, slot in partners:
+        @pl.when(jnp.logical_and(here + step >= 0, here + step < count))
+        def _():
+            copy(step, slot, here + step).start()
+    for step, slot in partners:
+        @pl.when(jnp.logical_and(here + step >= 0, here + step < count))
+        def _():
+            copy(step, slot, here + step).wait_send()
+        @pl.when(jnp.logical_and(here - step >= 0, here - step < count))
+        def _():
+            copy(step, slot, here - step).wait_recv()
+
+
+def lat_halo_kernel(block, width):
+    rows = block.shape[0]
+    far = width - rows
+    count = lax.axis_size("lat")
+    halo_shape = jax.ShapeDtypeStruct((width,) + block.shape[1:], block.dtype)
+    below, above = pl.pallas_call(
+        functools.partial(halo_body, count, rows, far),
+        out_shape=(halo_shape, halo_shape),
+        in_specs=[pl.BlockSpec(memory_space=pl.ANY)],
+        out_specs=(pl.BlockSpec(memory_space=pl.ANY), pl.BlockSpec(memory_space=pl.ANY)),
+        scratch_shapes=[pltpu.SemaphoreType.DMA((4,)), pltpu.SemaphoreType.DMA((4,))],
+        compiler_params=pltpu.CompilerParams(collective_id=0, has_side_effects=True),
+    )(block)
+    here = lax.axis_index("lat")
+    row = jnp.arange(width)[:, None, None]
+    below = jnp.where(jnp.where(row >= far, here >= 1, here >= 2), below, 0.0)
+    above = jnp.where(jnp.where(row < rows, here + 1 < count, here + 2 < count), above, 0.0)
+    return jnp.concatenate([below, block, above], axis=0)
+
+
 def shards(
     obs_values, obs_rows, obs_cols, row_frac, col_frac, obs_count, sigma, lat_scales, lon_scales
 ):
@@ -95,7 +157,7 @@
     departures = jnp.concatenate([(folded[0] + edge_row)[None], folded[1:tile_rows]], axis=0)
     weighted = departures * sigma
     half_width = HALF
-    window = lat_halo(weighted, half_width)
+    window = lat_halo_kernel(weighted, half_width)
     lat_kernel = kernel_matrix(lat_scales, tile_rows, half_width)
     lat_done = jnp.einsum(
         "lip,plc->ilc", lat_kernel, window, precision=lax.Precision.HIGH

time: 269 us -> 269 us (level)
  the two profiles are of different devices: /device:TPU:113 before, /device:TPU:265 now
where the time goes in v1:
time: 269 us; the launch traced here: 268 us
  Pallas kernels  171 us (64%)
  matrix products  38.6 us (14%)
  starting transfers between devices  18.2 us (7%)
  other arithmetic  15.9 us (6%)
  waiting for transfers between devices  12.4 us (5%)
  local copies, waits for them, and re-layouts  11.1 us (4%)
    pallas_call x1, Pallas kernels, lat_halo_kernel(): pl.pallas_call(functools.partial(halo_body, count, rows, far), out_shape=...  171 us
    dot_general x1, matrix products, shards(): jnp.einsum('krl,kc->rlc', row_values, col_w, precision=lax.Precision.HIGH)  29.1 us
    ppermute x1, starting transfers between devices, with_halo(): lax.ppermute(lax.slice_in_dim(block, block.shape[dim] - width, None, axis...  9.09 us
    ppermute x1, waiting for transfers between devices, with_halo(): lax.ppermute(lax.slice_in_dim(block, block.shape[dim] - width, None, axis...  6.63 us
    dot_general x1, matrix products, shards(): jnp.einsum('lip,plc->ilc', lat_kernel, window, precision=lax.Precision.HIGH)  6.07 us
  transfers between devices with their start and end apart: 4, of which 3 were waited for; matrix products, arithmetic and copies ran while one was open for 1% of the time, Pallas kernels for 0%

profile of v1, /device:TPU:265, one launch (start us, length us, event | category | flops | bytes accessed | tf_op | source)
XLA Modules:
  0.0 267.8 jit_solution(9016014345149226327)
XLA Ops:
  0.0 0.7 broadcast_add_fusion
  0.7 0.7 broadcast_subtract_fusion
  1.4 0.7 broadcast_add_fusion.1
  2.2 0.7 broadcast_subtract_fusion.1
  3.5 0.0 copy-start.5
  3.6 0.0 copy-start.6
  3.6 0.0 copy-start.4
  3.6 4.5 %fusion.59 = f32[4096,385,1]{0,1,2:T(8,128)} fusion(f32[4096]{0:T(1024)} %param.13, s32[4096]{0:T(1024)S(1)} %broadcast_add_fusion, f32[4096]{0:T(1024)S(1)} %broadcast_subtract_fusion, s32[4096]{0:T(1024)} %param.11), kind=kLoop, calls=%fused_computation.10.clone.2 | loop fusion | flops 7884800 | bytes 6373376 | tf_op jit(solution)/shard_map/krl,kc->rlc/dot_general | solution.py:149
  8.1 0.0 copy-done.5
  8.1 0.0 copy-done.6
  8.1 1.5 select_add_fusion
  9.6 0.0 copy-done.4
  9.6 29.1 %fusion = f32[97,16,385]{2,1,0:T(8,128)S(1)} fusion(f32[4096,16]{0,1:T(8,128)S(1)} %select_bitcast_fusion, f32[4096,97]{0,1:T(8,128)} %select_add_fusion, f32[4096,385,1]{0,1,2:T(8,128)} %fusion.59), kind=kOutput, calls=%fused_computation | convolution fusion | flops 14691008512 | bytes 10549312 | tf_op jit(solution)/shard_map/krl,kc->rlc/dot_general | solution.py:149
  38.7 0.0 copy-start.1
  38.7 0.0 copy-start.7
  38.7 0.0 copy-start.8
  38.7 1.4 fusion.51
  40.1 1.6 copy.34
  41.8 3.7 %collective-permute-start = (f32[97,16]{0,1:T(8,128)S(1)}, f32[97,16]{0,1:T(8,128)S(1)}, u32[]{:S(2)}, u32[]{:S(2)}) collective-permute-start(f32[97,16]{0,1:T(8,128)S(1)} %bitcast.48), channel_id=1, source_target_pairs={{15,0},{0,1},{1,2},{2,3},{3,4},{4,5},{5,6},{6,7},{7,8},{8,9},{9,10... | collective-permute-start | bytes 18632 | tf_op jit(solution)/shard_map/ppermute | solution.py:16
  45.6 0.0 copy-done.7
  45.6 0.0 copy-done.8
  45.6 0.2 fusion.44
  45.8 0.0 copy-done.1
  45.8 0.0 copy-start.2
  45.9 2.6 slice.44
  48.5 0.0 copy-done.2
  48.5 0.4 copy.33
  48.9 0.0 collective-permute-done
  48.9 0.5 copy.35
  49.4 0.1 maximum_bitcast_fusion
  49.4 0.0 copy-start.3
  49.4 3.3 %collective-permute-start.1 = (f32[16,384]{1,0:T(8,128)S(1)}, f32[16,384]{1,0:T(8,128)S(1)}, u32[]{:S(2)}, u32[]{:S(2)}) collective-permute-start(f32[16,384]{1,0:T(8,128)S(1)} %maximum_bitcast_fusion), channel_id=1, source_target_pairs={{0,16},{16,32},{32,48},{48,64},{64,80},{80,96},{96,112},{112,128},... | collective-permute-start | bytes 73736 | tf_op jit(solution)/shard_map/ppermute | solution.py:22
  52.8 1.3 collective-permute-done.1
  54.1 0.1 fusion.46
  54.2 0.0 copy-done.3
  54.2 2.2 fusion.27.x_ref
  56.4 170.5 %shard_map.91 = (f32[128,16,384]{2,1,0:T(8,128)}, f32[128,16,384]{2,1,0:T(8,128)}) custom-call(f32[96,16,384]{2,1,0:T(8,128)} %fusion.27.x_ref), custom_call_target="tpu_custom_call" | custom-call | tf_op jit(solution)/shard_map/pallas_call | solution.py:124
  226.9 0.0 copy-start
  226.9 3.4 %broadcast_select_fusion = (f32[128,16,384]{2,1,0:T(8,128)S(1)}, f32[128,16,384]{2,1,0:T(8,128)S(1)}) fusion(f32[128,16,384]{2,1,0:T(8,128)} %get-tuple-element.8, pred[128]{0:T(512)(128)(4,1)S(1)} %compare_select_fusion, f32[128,16,384]{2,1,0:T(8,128)} %get-tuple-element.7, pred[128]{0:T(512)(128)(4,1)S(1)} %compare_select_fusion.1), kind=kLoop, calls=%fused_computation.44 | loop fusion | flops 1572864 | bytes 12583168 | tf_op jit(solution)/shard_map/jit(_where)/select_n | solution.py:135
  230.3 0.1 copy-done
  230.4 0.6 pad_maximum_fusion
  231.0 6.1 %fusion.4 = f32[16,384,96]{1,2,0:T(8,128)S(1)} fusion(f32[352,16,384]{2,1,0:T(8,128)S(1)} %pad_maximum_fusion, f32[16]{0:T(128)S(1)} %sqrt.14, f32[16]{0:T(128)S(1)} %get-tuple-element.19, f32[96,352]{1,0:T(8,128)S(1)} %multiply_negate_fusion.1, pred[96,352]{1,0:T(8,128)(4,1)S(1)} %abs_compare_fusion.1), kind=kOutput, calls=%fused_computation.5 | convolution fusion | flops 1247330304 | bytes 11179136 | tf_op jit(solution)/shard_map/lip,plc->ilc/dot_general | solution.py:162
  237.1 0.2 fusion.52
  237.3 9.1 %collective-permute-start.2 = (f32[96,16,128]{2,0,1:T(8,128)S(1)}, f32[96,16,128]{2,0,1:T(8,128)S(1)}, u32[]{:S(2)}, u32[]{:S(2)}) collective-permute-start(f32[96,16,128]{2,0,1:T(8,128)S(1)} %get-tuple-element.15), channel_id=1, source_target_pairs={{0,1},{1,2},{2,3},{3,4},{4,5},{5,6},{6,7},{7,8},{8,9},{9,10},{10,1... | collective-permute-start | bytes 2359304 | tf_op jit(solution)/shard_map/ppermute | solution.py:31
  246.4 2.1 collective-permute-start.3
  248.6 0.1 abs_compare_fusion
  248.7 6.6 %collective-permute-done.2 = f32[96,16,128]{2,0,1:T(8,128)S(1)} collective-permute-done((f32[96,16,128]{2,0,1:T(8,128)S(1)}, f32[96,16,128]{2,0,1:T(8,128)S(1)}, u32[]{:S(2)}, u32[]{:S(2)}) %collective-permute-start.2) | collective-permute-done | bytes 786464 | tf_op jit(solution)/shard_map/ppermute | solution.py:31
  255.3 4.4 %collective-permute-done.3 = f32[96,16,128]{2,0,1:T(8,128)S(1)} collective-permute-done((f32[96,16,128]{2,0,1:T(8,128)S(1)}, f32[96,16,128]{2,0,1:T(8,128)S(1)}, u32[]{:S(2)}, u32[]{:S(2)}) %collective-permute-start.3) | collective-permute-done | bytes 786464 | tf_op jit(solution)/shard_map/ppermute | solution.py:34
  259.7 0.4 fusion.25
  260.1 3.5 %fusion.28 = f32[96,16,3,128]{3,0,2,1:T(8,128)S(1)} fusion(f32[16]{0:T(128)S(1)} %sqrt.15, f32[16]{0:T(128)S(1)} %get-tuple-element.17, f32[128,384]{1,0:T(8,128)S(1)} %multiply_negate_fusion, pred[128,384]{1,0:T(8,128)(4,1)S(1)} %abs_compare_fusion, f32[96,16,1,384]{3,0,1,2:T(8,128)S(1)} %get-tuple-element.14, f32[96,16,1,384]{3,0,1,2:T(8,128)S(1)} %bitcast.47, ...), kind=kOutput, calls=%fused_computation.39 | convolution fusion | flops 1364852736 | bytes 9683072 | tf_op jit(solution)/shard_map/lip,rlbp->rlbi/dot_general | solution.py:173
  263.6 1.6 copy.38
  265.2 2.6 reshape.226
  (15 shorter events, 0.2 us)
Async XLA Ops:
  3.5 4.5 %copy-start.5 = (f32[4096]{0:T(1024)S(1)}, f32[4096]{0:T(1024)}, u32[]{:S(2)}) copy-start(f32[4096]{0:T(1024)} %param.12) | copy-start | bytes 49156
  3.6 4.5 %copy-start.6 = (s32[4096]{0:T(1024)S(1)}, s32[4096]{0:T(1024)}, u32[]{:S(2)}) copy-start(s32[4096]{0:T(1024)} %param.10) | copy-start | bytes 49156
  3.6 6.0 %copy-start.4 = (f32[16,4096]{1,0:T(8,128)S(1)}, f32[16,4096]{1,0:T(8,128)}, u32[]{:S(2)}) copy-start(f32[16,4096]{1,0:T(8,128)} %param.9) | copy-start | bytes 786436
  38.7 7.2 %copy-start.1 = (f32[97,16,385]{2,1,0:T(8,128)}, f32[97,16,385]{2,1,0:T(8,128)S(1)}, u32[]{:S(2)}) copy-start(f32[97,16,385]{2,1,0:T(8,128)S(1)} %fusion) | copy-start | bytes 7170244
  38.7 6.9 %copy-start.7 = (f32[16]{0:T(128)S(1)}, f32[16]{0:T(128)}, u32[]{:S(2)}) copy-start(f32[16]{0:T(128)} %param.17) | copy-start | bytes 196
  38.7 6.9 %copy-start.8 = (f32[16]{0:T(128)S(1)}, f32[16]{0:T(128)}, u32[]{:S(2)}) copy-start(f32[16]{0:T(128)} %param.16) | copy-start | bytes 196
  41.8 7.1 %collective-permute-start = (f32[97,16]{0,1:T(8,128)S(1)}, f32[97,16]{0,1:T(8,128)S(1)}, u32[]{:S(2)}, u32[]{:S(2)}) collective-permute-start(f32[97,16]{0,1:T(8,128)S(1)} %bitcast.48), channel_id=1, source_target_pairs={{15,0},{0,1},{1,2},{2,3},{3,4},{4,5},{5,6},{6,7},{7,8},{8,9},{9,10... | collective-permute-start | bytes 18632 | tf_op jit(solution)/shard_map/ppermute | solution.py:16
  45.8 2.7 copy-start.2
  49.4 4.8 %copy-start.3 = (f32[96,16,384]{2,1,0:T(8,128)S(1)}, f32[96,16,384]{2,1,0:T(8,128)}, u32[]{:S(2)}) copy-start(f32[96,16,384]{2,1,0:T(8,128)} %param.15) | copy-start | bytes 7077892
  49.4 4.7 %collective-permute-start.1 = (f32[16,384]{1,0:T(8,128)S(1)}, f32[16,384]{1,0:T(8,128)S(1)}, u32[]{:S(2)}, u32[]{:S(2)}) collective-permute-start(f32[16,384]{1,0:T(8,128)S(1)} %maximum_bitcast_fusion), channel_id=1, source_target_pairs={{0,16},{16,32},{32,48},{48,64},{64,80},{80,96},{96,112},{112,128},... | collective-permute-start | bytes 73736 | tf_op jit(solution)/shard_map/ppermute | solution.py:22
  226.9 3.5 %copy-start = (f32[96,16,384]{2,1,0:T(8,128)S(1)}, f32[96,16,384]{2,1,0:T(8,128)}, u32[]{:S(2)}) copy-start(f32[96,16,384]{2,1,0:T(8,128)} %fusion.27.x_ref) | copy-start | bytes 7077892
  237.3 18.0 %collective-permute-start.2 = (f32[96,16,128]{2,0,1:T(8,128)S(1)}, f32[96,16,128]{2,0,1:T(8,128)S(1)}, u32[]{:S(2)}, u32[]{:S(2)}) collective-permute-start(f32[96,16,128]{2,0,1:T(8,128)S(1)} %get-tuple-element.15), channel_id=1, source_target_pairs={{0,1},{1,2},{2,3},{3,4},{4,5},{5,6},{6,7},{7,8},{8,9},{9,10},{10,1... | collective-permute-start | bytes 2359304 | tf_op jit(solution)/shard_map/ppermute | solution.py:31
  246.4 13.3 %collective-permute-start.3 = (f32[96,16,128]{2,0,1:T(8,128)S(1)}, f32[96,16,128]{2,0,1:T(8,128)S(1)}, u32[]{:S(2)}, u32[]{:S(2)}) collective-permute-start(f32[96,16,128]{2,0,1:T(8,128)S(1)} %get-tuple-element.16), channel_id=1, source_target_pairs={{1,0},{2,1},{3,2},{4,3},{5,4},{6,5},{7,6},{8,7},{9,8},{10,9},{11,1... | collective-permute-start | bytes 2359304 | tf_op jit(solution)/shard_map/ppermute | solution.py:34

commit v2 on v0

--- a/solution.py
+++ b/solution.py
@@ -1,6 +1,10 @@
+import functools
+
 import jax
 import jax.numpy as jnp
 from jax import lax
+from jax.experimental import pallas as pl
+from jax.experimental.pallas import tpu as pltpu
 from jax.sharding import PartitionSpec as P
 
 HALF = 128
@@ -74,7 +78,110 @@
     return jnp.concatenate(parts, axis=0)
 
 
+def relay_halo_body(count, span, rows, far, x_ref, below_ref, above_ref, relay_ref, send_sem, recv_sem):
+    here = lax.axis_index("lat")
+    column = lax.axis_index("lon")
+    mesh = pl.DeviceIdType.MESH
+    half = x_ref.shape[1] // 2
+    last = span - 1
+    first_of = here % span == 0
+    last_of = here % span == last
+    up_exists = here + 1 < count
+    down_exists = here >= 1
+    cross_up = jnp.logical_and(up_exists, (here + 1) % span == 0)
+    cross_down = jnp.logical_and(down_exists, first_of)
+    low, high = pl.ds(0, half), pl.ds(half, half)
+    near_below = below_ref.at[pl.ds(far, rows)]
+    near_above = above_ref.at[pl.ds(0, rows)]
+    plan = {
+        0: (here + 2 < count, 2, x_ref.at[pl.ds(rows - far, far)], below_ref.at[pl.ds(0, far)], here >= 2),
+        1: (here >= 2, -2, x_ref.at[pl.ds(0, far)], above_ref.at[pl.ds(rows, far)], here + 2 < count),
+        2: (jnp.logical_and(up_exists, jnp.logical_not(cross_up)), 1, x_ref, near_below,
+            jnp.logical_and(down_exists, jnp.logical_not(first_of))),
+        3: (jnp.logical_and(down_exists, jnp.logical_not(first_of)), -1, x_ref, near_above,
+            jnp.logical_and(up_exists, jnp.logical_not(cross_up))),
+        4: (cross_up, span, x_ref.at[:, low], relay_ref.at[0], jnp.logical_and(last_of, here >= span)),
+        5: (cross_up, 1 - span, x_ref.at[:, high], relay_ref.at[1], jnp.logical_and(first_of, here + span < count)),
+        6: (cross_down, -span, x_ref.at[:, low], relay_ref.at[2], jnp.logical_and(first_of, here + span < count)),
+        7: (cross_down, span - 1, x_ref.at[:, high], relay_ref.at[3], jnp.logical_and(last_of, here >= span)),
+        8: (jnp.logical_and(last_of, here >= span), 1 - span, relay_ref.at[0], near_below.at[:, low],
+            jnp.logical_and(first_of, here >= span)),
+        9: (jnp.logical_and(first_of, here + span < count), span, relay_ref.at[1], near_below.at[:, high],
+            jnp.logical_and(first_of, here >= span)),
+        10: (jnp.logical_and(first_of, here + span < count), span - 1, relay_ref.at[2], near_above.at[:, low],
+             jnp.logical_and(last_of, up_exists)),
+        11: (jnp.logical_and(last_of, here >= span), -span, relay_ref.at[3], near_above.at[:, high],
+             jnp.logical_and(last_of, up_exists)),
+    }
+    feeds = {8: 4, 9: 5, 10: 6, 11: 7}
+
+    barrier = pltpu.get_barrier_semaphore()
+    offsets = sorted({offset for _, offset, _, _, _ in plan.values()})
+    for offset in offsets:
+        neighbour = lax.rem(here + offset + count, count)
+        pl.semaphore_signal(barrier, 1, device_id=(neighbour, column), device_id_type=mesh)
+    pl.semaphore_wait(barrier, len(offsets))
+
+    def copy(slot, device):
+        _, _, src, dst, _ = plan[slot]
+        return pltpu.make_async_remote_copy(
+            src_ref=src, dst_ref=dst, send_sem=send_sem.at[slot], recv_sem=recv_sem.at[slot],
+            device_id=(device, column), device_id_type=mesh,
+        )
+
+    def when_start(slot):
+        sends, offset, _, _, _ = plan[slot]
+
+        @pl.when(sends)
+        def _():
+            copy(slot, here + offset).start()
+
+    for slot in range(8):
+        when_start(slot)
+    for slot, source in feeds.items():
+        @pl.when(plan[slot][0])
+        def _():
+            copy(source, here).wait_recv()
+            copy(slot, here + plan[slot][1]).start()
+    for slot in range(12):
+        sends, offset, _, _, receives = plan[slot]
+
+        @pl.when(sends)
+        def _():
+            copy(slot, here + offset).wait_send()
+
+        if slot in feeds.values():
+            continue
+
+        @pl.when(receives)
+        def _():
+            copy(slot, here).wait_recv()
+
+
+def lat_halo_kernel(block, width, span):
+    rows = block.shape[0]
+    far = width - rows
+    count = lax.axis_size("lat")
+    halo_shape = jax.ShapeDtypeStruct((width,) + block.shape[1:], block.dtype)
+    levels = block.shape[1]
+    relay_shape = jax.ShapeDtypeStruct((4, rows, levels // 2, block.shape[2]), block.dtype)
+    below, above, _ = pl.pallas_call(
+        functools.partial(relay_halo_body, count, span, rows, far),
+        out_shape=(halo_shape, halo_shape, relay_shape),
+        in_specs=[pl.BlockSpec(memory_space=pl.ANY)],
+        out_specs=(pl.BlockSpec(memory_space=pl.ANY),) * 3,
+        scratch_shapes=[pltpu.SemaphoreType.DMA((12,)), pltpu.SemaphoreType.DMA((12,))],
+        compiler_params=pltpu.CompilerParams(collective_id=0, has_side_effects=True),
+    )(block)
+    here = lax.axis_index("lat")
+    row = jnp.arange(width)[:, None, None]
+    below = jnp.where(jnp.where(row >= far, here >= 1, here >= 2), below, 0.0)
+    above = jnp.where(jnp.where(row < rows, here + 1 < count, here + 2 < count), above, 0.0)
+    return jnp.concatenate([below, block, above], axis=0)
+
+
 def shards(
+    span,
     obs_values, obs_rows, obs_cols, row_frac, col_frac, obs_count, sigma, lat_scales, lon_scales
 ):
     tile_rows, level_count, tile_cols = sigma.shape
@@ -95,7 +202,7 @@
     departures = jnp.concatenate([(folded[0] + edge_row)[None], folded[1:tile_rows]], axis=0)
     weighted = departures * sigma
     half_width = HALF
-    window = lat_halo(weighted, half_width)
+    window = lat_halo_kernel(weighted, half_width, span)
     lat_kernel = kernel_matrix(lat_scales, tile_rows, half_width)
     lat_done = jnp.einsum(
         "lip,plc->ilc", lat_kernel, window, precision=lax.Precision.HIGH
@@ -112,6 +219,14 @@
     return result.reshape(tile_rows, level_count, tile_cols)
 
 
+def lat_groups(mesh):
+    column = mesh.devices[:, 0]
+    coords = [getattr(device, "coords", None) for device in column]
+    if any(c is None for c in coords):
+        return tuple(index // 8 for index in range(len(column)))
+    return tuple(c[2] // 2 for c in coords)
+
+
 def solution(mesh):
     in_specs = (
         P(None, ("lat", "lon")),
@@ -125,4 +240,6 @@
         P(),
     )
     out_specs = P("lat", None, "lon")
-    return jax.shard_map(shards, mesh=mesh, in_specs=in_specs, out_specs=out_specs, check_vma=False)
+    groups = lat_groups(mesh)
+    span = groups.index(groups[0] + 1) if groups[0] + 1 in groups else len(groups)
+    return jax.shard_map(functools.partial(shards, span), mesh=mesh, in_specs=in_specs, out_specs=out_specs, check_vma=False)

time: 269 us -> 218 us (0.81)
  the two profiles are of different devices: /device:TPU:113 before, /device:TPU:57 now
where the time goes in v2:
time: 218 us
  Pallas kernels  122 us (56%)
  matrix products  38.6 us (18%)
  starting transfers between devices  16.6 us (8%)
  other arithmetic  15.9 us (7%)
  waiting for transfers between devices  11.9 us (5%)
  local copies, waits for them, and re-layouts  11.1 us (5%)
    pallas_call x1, Pallas kernels, lat_halo_kernel(): pl.pallas_call(functools.partial(relay_halo_body, count, span, rows, far)...  122 us
    dot_general x1, matrix products, shards(): jnp.einsum('krl,kc->rlc', row_values, col_w, precision=lax.Precision.HIGH)  29.1 us
    ppermute x1, waiting for transfers between devices, with_halo(): lax.ppermute(lax.slice_in_dim(block, block.shape[dim] - width, None, axis...  6.63 us
    dot_general x1, matrix products, shards(): jnp.einsum('lip,plc->ilc', lat_kernel, window, precision=lax.Precision.HIGH)  6.07 us
    ppermute x1, starting transfers between devices, with_halo(): lax.ppermute(lax.slice_in_dim(block, block.shape[dim] - width, None, axis...  5.67 us
    ppermute x1, starting transfers between devices, shifted(): return lax.ppermute(block, axis, route)  5.14 us
    dot_general x1, other arithmetic, shards(): jnp.einsum('krl,kc->rlc', row_values, col_w, precision=lax.Precision.HIGH)  4.51 us
    ppermute x1, waiting for transfers between devices, with_halo(): lax.ppermute(lax.slice_in_dim(block, 0, width, axis=dim), axis, backward)  4.4 us
  transfers between devices with their start and end apart: 4, of which 3 were waited for; matrix products, arithmetic and copies ran while one was open for 2% of the time, Pallas kernels for 0%

profile of v2, /device:TPU:57, one launch (start us, length us, event | category | flops | bytes accessed | tf_op | source)
XLA Modules:
  0.0 217.7 jit_solution(9748521689958173381)
XLA Ops:
  0.0 0.7 broadcast_add_fusion
  0.7 0.7 broadcast_subtract_fusion
  1.4 0.7 broadcast_add_fusion.1
  2.2 0.7 broadcast_subtract_fusion.1
  3.5 0.0 copy-start.5
  3.6 0.0 copy-start.6
  3.6 0.0 copy-start.4
  3.6 4.5 %fusion.59 = f32[4096,385,1]{0,1,2:T(8,128)} fusion(f32[4096]{0:T(1024)} %param.13, s32[4096]{0:T(1024)S(1)} %broadcast_add_fusion, f32[4096]{0:T(1024)S(1)} %broadcast_subtract_fusion, s32[4096]{0:T(1024)} %param.11), kind=kLoop, calls=%fused_computation.10.clone.2 | loop fusion | flops 7884800 | bytes 6373376 | tf_op jit(solution)/shard_map/krl,kc->rlc/dot_general | solution.py:194
  8.1 0.0 copy-done.5
  8.1 0.0 copy-done.6
  8.1 1.5 select_add_fusion
  9.6 0.0 copy-done.4
  9.6 29.1 %fusion = f32[97,16,385]{2,1,0:T(8,128)S(1)} fusion(f32[4096,16]{0,1:T(8,128)S(1)} %select_bitcast_fusion, f32[4096,97]{0,1:T(8,128)} %select_add_fusion, f32[4096,385,1]{0,1,2:T(8,128)} %fusion.59), kind=kOutput, calls=%fused_computation | convolution fusion | flops 14691008512 | bytes 10549312 | tf_op jit(solution)/shard_map/krl,kc->rlc/dot_general | solution.py:194
  38.7 0.0 copy-start.1
  38.7 0.0 copy-start.7
  38.7 0.0 copy-start.8
  38.7 1.4 fusion.51
  40.2 1.6 copy.34
  41.8 3.7 %collective-permute-start = (f32[97,16]{0,1:T(8,128)S(1)}, f32[97,16]{0,1:T(8,128)S(1)}, u32[]{:S(2)}, u32[]{:S(2)}) collective-permute-start(f32[97,16]{0,1:T(8,128)S(1)} %bitcast.48), channel_id=1, source_target_pairs={{15,0},{0,1},{1,2},{2,3},{3,4},{4,5},{5,6},{6,7},{7,8},{8,9},{9,10... | collective-permute-start | bytes 18632 | tf_op jit(solution)/shard_map/ppermute | solution.py:16
  45.6 0.0 copy-done.7
  45.6 0.0 copy-done.8
  45.6 0.2 fusion.44
  45.8 0.0 copy-done.1
  45.8 0.0 copy-start.2
  45.9 2.6 %slice.44 = f32[97,16,383]{2,1,0:T(8,128)S(1)} slice(f32[97,16,385]{2,1,0:T(8,128)} %copy-done.1), slice={[0:97], [0:16], [1:384]} | slice | bytes 4755328 | tf_op jit(solution)/shard_map/slice | solution.py:199
  48.5 0.0 copy-done.2
  48.5 0.4 copy.33
  48.9 0.0 collective-permute-done
  48.9 0.5 copy.35
  49.4 0.1 maximum_bitcast_fusion
  49.4 0.0 copy-start.3
  49.4 5.1 %collective-permute-start.1 = (f32[16,384]{1,0:T(8,128)S(1)}, f32[16,384]{1,0:T(8,128)S(1)}, u32[]{:S(2)}, u32[]{:S(2)}) collective-permute-start(f32[16,384]{1,0:T(8,128)S(1)} %maximum_bitcast_fusion), channel_id=1, source_target_pairs={{0,16},{16,32},{32,48},{48,64},{64,80},{80,96},{96,112},{112,128},... | collective-permute-start | bytes 73736 | tf_op jit(solution)/shard_map/ppermute | solution.py:22
  54.6 0.9 collective-permute-done.1
  55.5 0.1 fusion.46
  55.6 0.0 copy-done.3
  55.6 2.2 fusion.27.x_ref
  57.8 122.5 %shard_map.91 = (f32[128,16,384]{2,1,0:T(8,128)}, f32[128,16,384]{2,1,0:T(8,128)}, f32[4,96,8,384]{3,2,1,0:T(8,128)}) custom-call(f32[96,16,384]{2,1,0:T(8,128)} %fusion.27.x_ref), custom_call_target="tpu_custom_call" | custom-call | tf_op jit(solution)/shard_map/pallas_call | solution.py:168
  180.2 0.0 copy-start
  180.2 3.4 %broadcast_select_fusion = (f32[128,16,384]{2,1,0:T(8,128)S(1)}, f32[128,16,384]{2,1,0:T(8,128)S(1)}) fusion(f32[128,16,384]{2,1,0:T(8,128)} %get-tuple-element.8, pred[128]{0:T(512)(128)(4,1)S(1)} %compare_select_fusion, f32[128,16,384]{2,1,0:T(8,128)} %get-tuple-element.7, pred[128]{0:T(512)(128)(4,1)S(1)} %compare_select_fusion.1), kind=kLoop, calls=%fused_computation.44 | loop fusion | flops 1572864 | bytes 12583168 | tf_op jit(solution)/shard_map/jit(_where)/select_n | solution.py:179
  183.6 0.1 copy-done
  183.8 0.6 pad_maximum_fusion
  184.4 6.1 %fusion.4 = f32[16,384,96]{1,2,0:T(8,128)S(1)} fusion(f32[352,16,384]{2,1,0:T(8,128)S(1)} %pad_maximum_fusion, f32[16]{0:T(128)S(1)} %sqrt.14, f32[16]{0:T(128)S(1)} %get-tuple-element.19, f32[96,352]{1,0:T(8,128)S(1)} %multiply_negate_fusion.1, pred[96,352]{1,0:T(8,128)(4,1)S(1)} %abs_compare_fusion.1), kind=kOutput, calls=%fused_computation.5 | convolution fusion | flops 1247330304 | bytes 11179136 | tf_op jit(solution)/shard_map/lip,plc->ilc/dot_general | solution.py:207
  190.4 0.2 fusion.52
  190.6 5.7 %collective-permute-start.2 = (f32[96,16,128]{2,0,1:T(8,128)S(1)}, f32[96,16,128]{2,0,1:T(8,128)S(1)}, u32[]{:S(2)}, u32[]{:S(2)}) collective-permute-start(f32[96,16,128]{2,0,1:T(8,128)S(1)} %get-tuple-element.15), channel_id=1, source_target_pairs={{0,1},{1,2},{2,3},{3,4},{4,5},{5,6},{6,7},{7,8},{8,9},{9,10},{10,1... | collective-permute-start | bytes 2359304 | tf_op jit(solution)/shard_map/ppermute | solution.py:31
  196.3 2.1 collective-permute-start.3
  198.5 0.1 abs_compare_fusion
  198.6 6.6 %collective-permute-done.2 = f32[96,16,128]{2,0,1:T(8,128)S(1)} collective-permute-done((f32[96,16,128]{2,0,1:T(8,128)S(1)}, f32[96,16,128]{2,0,1:T(8,128)S(1)}, u32[]{:S(2)}, u32[]{:S(2)}) %collective-permute-start.2) | collective-permute-done | bytes 786464 | tf_op jit(solution)/shard_map/ppermute | solution.py:31
  205.2 4.4 %collective-permute-done.3 = f32[96,16,128]{2,0,1:T(8,128)S(1)} collective-permute-done((f32[96,16,128]{2,0,1:T(8,128)S(1)}, f32[96,16,128]{2,0,1:T(8,128)S(1)}, u32[]{:S(2)}, u32[]{:S(2)}) %collective-permute-start.3) | collective-permute-done | bytes 786464 | tf_op jit(solution)/shard_map/ppermute | solution.py:34
  209.6 0.4 fusion.25
  210.0 3.5 %fusion.28 = f32[96,16,3,128]{3,0,2,1:T(8,128)S(1)} fusion(f32[16]{0:T(128)S(1)} %sqrt.15, f32[16]{0:T(128)S(1)} %get-tuple-element.17, f32[128,384]{1,0:T(8,128)S(1)} %multiply_negate_fusion, pred[128,384]{1,0:T(8,128)(4,1)S(1)} %abs_compare_fusion, f32[96,16,1,384]{3,0,1,2:T(8,128)S(1)} %get-tuple-element.14, f32[96,16,1,384]{3,0,1,2:T(8,128)S(1)} %bitcast.47, ...), kind=kOutput, calls=%fused_computation.39 | convolution fusion | flops 1364852736 | bytes 9683072 | tf_op jit(solution)/shard_map/lip,rlbp->rlbi/dot_general | solution.py:218
  213.5 1.6 copy.38
  215.1 2.6 %reshape.226 = f32[96,16,384]{2,1,0:T(8,128)} reshape(f32[96,16,3,128]{3,2,1,0:T(4,128)S(1)} %copy.38) | data formatting | bytes 4718592 | tf_op jit(solution)/shard_map/reshape | solution.py:219
  (15 shorter events, 0.2 us)
Async XLA Ops:
  3.5 4.5 %copy-start.5 = (f32[4096]{0:T(1024)S(1)}, f32[4096]{0:T(1024)}, u32[]{:S(2)}) copy-start(f32[4096]{0:T(1024)} %param.12) | copy-start | bytes 49156
  3.6 4.5 %copy-start.6 = (s32[4096]{0:T(1024)S(1)}, s32[4096]{0:T(1024)}, u32[]{:S(2)}) copy-start(s32[4096]{0:T(1024)} %param.10) | copy-start | bytes 49156
  3.6 6.0 %copy-start.4 = (f32[16,4096]{1,0:T(8,128)S(1)}, f32[16,4096]{1,0:T(8,128)}, u32[]{:S(2)}) copy-start(f32[16,4096]{1,0:T(8,128)} %param.9) | copy-start | bytes 786436
  38.7 7.1 %copy-start.1 = (f32[97,16,385]{2,1,0:T(8,128)}, f32[97,16,385]{2,1,0:T(8,128)S(1)}, u32[]{:S(2)}) copy-start(f32[97,16,385]{2,1,0:T(8,128)S(1)} %fusion) | copy-start | bytes 7170244
  38.7 6.9 %copy-start.7 = (f32[16]{0:T(128)S(1)}, f32[16]{0:T(128)}, u32[]{:S(2)}) copy-start(f32[16]{0:T(128)} %param.17) | copy-start | bytes 196
  38.7 6.9 %copy-start.8 = (f32[16]{0:T(128)S(1)}, f32[16]{0:T(128)}, u32[]{:S(2)}) copy-start(f32[16]{0:T(128)} %param.16) | copy-start | bytes 196
  41.8 7.1 %collective-permute-start = (f32[97,16]{0,1:T(8,128)S(1)}, f32[97,16]{0,1:T(8,128)S(1)}, u32[]{:S(2)}, u32[]{:S(2)}) collective-permute-start(f32[97,16]{0,1:T(8,128)S(1)} %bitcast.48), channel_id=1, source_target_pairs={{15,0},{0,1},{1,2},{2,3},{3,4},{4,5},{5,6},{6,7},{7,8},{8,9},{9,10... | collective-permute-start | bytes 18632 | tf_op jit(solution)/shard_map/ppermute | solution.py:16
  45.8 2.7 %copy-start.2 = (f32[97,16,1]{2,1,0:T(8,128)S(1)}, f32[97,16,1]{2,1,0:T(8,128)}, u32[]{:S(2)}) copy-start(f32[97,16,1]{2,1,0:T(8,128)} %get-tuple-element.11) | copy-start | bytes 18628
  49.4 6.2 %copy-start.3 = (f32[96,16,384]{2,1,0:T(8,128)S(1)}, f32[96,16,384]{2,1,0:T(8,128)}, u32[]{:S(2)}) copy-start(f32[96,16,384]{2,1,0:T(8,128)} %param.15) | copy-start | bytes 7077892
  49.4 6.1 %collective-permute-start.1 = (f32[16,384]{1,0:T(8,128)S(1)}, f32[16,384]{1,0:T(8,128)S(1)}, u32[]{:S(2)}, u32[]{:S(2)}) collective-permute-start(f32[16,384]{1,0:T(8,128)S(1)} %maximum_bitcast_fusion), channel_id=1, source_target_pairs={{0,16},{16,32},{32,48},{48,64},{64,80},{80,96},{96,112},{112,128},... | collective-permute-start | bytes 73736 | tf_op jit(solution)/shard_map/ppermute | solution.py:22
  180.2 3.5 %copy-start = (f32[96,16,384]{2,1,0:T(8,128)S(1)}, f32[96,16,384]{2,1,0:T(8,128)}, u32[]{:S(2)}) copy-start(f32[96,16,384]{2,1,0:T(8,128)} %fusion.27.x_ref) | copy-start | bytes 7077892
  190.6 14.6 %collective-permute-start.2 = (f32[96,16,128]{2,0,1:T(8,128)S(1)}, f32[96,16,128]{2,0,1:T(8,128)S(1)}, u32[]{:S(2)}, u32[]{:S(2)}) collective-permute-start(f32[96,16,128]{2,0,1:T(8,128)S(1)} %get-tuple-element.15), channel_id=1, source_target_pairs={{0,1},{1,2},{2,3},{3,4},{4,5},{5,6},{6,7},{7,8},{8,9},{9,10},{10,1... | collective-permute-start | bytes 2359304 | tf_op jit(solution)/shard_map/ppermute | solution.py:31
  196.3 13.3 %collective-permute-start.3 = (f32[96,16,128]{2,0,1:T(8,128)S(1)}, f32[96,16,128]{2,0,1:T(8,128)S(1)}, u32[]{:S(2)}, u32[]{:S(2)}) collective-permute-start(f32[96,16,128]{2,0,1:T(8,128)S(1)} %get-tuple-element.16), channel_id=1, source_target_pairs={{1,0},{2,1},{3,2},{4,3},{5,4},{6,5},{7,6},{8,7},{9,8},{10,9},{11,1... | collective-permute-start | bytes 2359304 | tf_op jit(solution)/shard_map/ppermute | solution.py:34

commit v3 on v2

--- a/solution.py
+++ b/solution.py
@@ -180,6 +180,49 @@
     return jnp.concatenate([below, block, above], axis=0)
 
 
+def lon_halo_body(count, width, x_ref, west_ref, east_ref, send_sem, recv_sem):
+    here = lax.axis_index("lon")
+    row = lax.axis_index("lat")
+    mesh = pl.DeviceIdType.MESH
+    cols = x_ref.shape[2]
+    east = lax.rem(here + 1, count)
+    west = lax.rem(here + count - 1, count)
+    barrier = pltpu.get_barrier_semaphore()
+    for neighbour in (west, east):
+        pl.semaphore_signal(barrier, 1, device_id=(row, neighbour), device_id_type=mesh)
+    pl.semaphore_wait(barrier, 2)
+    copies = [
+        pltpu.make_async_remote_copy(
+            src_ref=x_ref.at[:, :, pl.ds(cols - width, width)], dst_ref=west_ref,
+            send_sem=send_sem.at[0], recv_sem=recv_sem.at[0],
+            device_id=(row, east), device_id_type=mesh,
+        ),
+        pltpu.make_async_remote_copy(
+            src_ref=x_ref.at[:, :, pl.ds(0, width)], dst_ref=east_ref,
+            send_sem=send_sem.at[1], recv_sem=recv_sem.at[1],
+            device_id=(row, west), device_id_type=mesh,
+        ),
+    ]
+    for copy in copies:
+        copy.start()
+    for copy in copies:
+        copy.wait()
+
+
+def lon_halo_kernel(block, width):
+    count = lax.axis_size("lon")
+    edge = jax.ShapeDtypeStruct(block.shape[:2] + (width,), block.dtype)
+    west, east = pl.pallas_call(
+        functools.partial(lon_halo_body, count, width),
+        out_shape=(edge, edge),
+        in_specs=[pl.BlockSpec(memory_space=pl.ANY)],
+        out_specs=(pl.BlockSpec(memory_space=pl.ANY),) * 2,
+        scratch_shapes=[pltpu.SemaphoreType.DMA((2,)), pltpu.SemaphoreType.DMA((2,))],
+        compiler_params=pltpu.CompilerParams(collective_id=1, has_side_effects=True),
+    )(block)
+    return jnp.concatenate([west, block, east], axis=2)
+
+
 def shards(
     span,
     obs_values, obs_rows, obs_cols, row_frac, col_frac, obs_count, sigma, lat_scales, lon_scales
@@ -207,7 +250,7 @@
     lat_done = jnp.einsum(
         "lip,plc->ilc", lat_kernel, window, precision=lax.Precision.HIGH
     )
-    padded_cols = with_halo(lat_done, (("lon", 2),), half_width)
+    padded_cols = lon_halo_kernel(lat_done, half_width)
     band = half_width
     lon_kernel = kernel_matrix(lon_scales, band, half_width)
     band_count = tile_cols // band

time: 218 us -> 226 us (1.037)
  Pallas kernels: 122 us -> 137 us
  waiting for transfers between devices: 11.9 us -> 0.01 us
  starting transfers between devices: 16.6 us -> 8.81 us
  local copies, waits for them, and re-layouts: 11.1 us -> 15.5 us
  other arithmetic: 15.9 us -> 20.2 us
  matrix products: 38.6 us -> 41.1 us
    pallas_call x0 -> x1, Pallas kernels: none -> 13.7 us  [lon_halo_kernel(): pl.pallas_call(functools.partial(lon_halo_body, count, width), out_shape=...]
    ppermute x2 -> x0, waiting for transfers between devices: 11 us -> none  [the longest x1 6.63 us: with_halo(): lax.ppermute(lax.slice_in_dim(block, block.shape[dim] - width, None, axis...]
    ppermute x2 -> x0, starting transfers between devices: 7.81 us -> none  [the longest x1 5.67 us: with_halo(): lax.ppermute(lax.slice_in_dim(block, block.shape[dim] - width, None, axis...]
    dot_general x0 -> x1, local copies, waits for them, and re-layouts: none -> 2.77 us  [shards(): jnp.einsum('lip,plc->ilc', lat_kernel, window, precision=lax.Precision.HIGH)]
    dot_general x1, matrix products: 3.48 us -> 5.94 us  [shards(): jnp.einsum('lip,rlbp->rlbi', lon_kernel, bands, precision=lax.Precision.H...]
  transfers between devices with their start and end apart: 4 -> 2, of which waited for: 3 -> 0; matrix products, arithmetic and copies ran while one was open for 2% -> 3% of each run, Pallas kernels for 0% -> 0%
where the time goes in v3:
time: 226 us; the launch traced here: 223 us
  Pallas kernels  137 us (61%)
  matrix products  41.1 us (18%)
  other arithmetic  20.2 us (9%)
  local copies, waits for them, and re-layouts  15.5 us (7%)
  starting transfers between devices  8.81 us (4%)
    pallas_call x1, Pallas kernels, lat_halo_kernel(): pl.pallas_call(functools.partial(relay_halo_body, count, span, rows, far)...  123 us
    dot_general x1, matrix products, shards(): jnp.einsum('krl,kc->rlc', row_values, col_w, precision=lax.Precision.HIGH)  29.1 us
    pallas_call x1, Pallas kernels, lon_halo_kernel(): pl.pallas_call(functools.partial(lon_halo_body, count, width), out_shape=...  13.7 us
    dot_general x1, matrix products, shards(): jnp.einsum('lip,plc->ilc', lat_kernel, window, precision=lax.Precision.HIGH)  6.07 us
    dot_general x1, matrix products, shards(): jnp.einsum('lip,rlbp->rlbi', lon_kernel, bands, precision=lax.Precision.H...  5.94 us
    ppermute x1, starting transfers between devices, shifted(): return lax.ppermute(block, axis, route)  5.14 us
  transfers between devices with their start and end apart: 2, of which 0 were waited for; matrix products, arithmetic and copies ran while one was open for 3% of the time, Pallas kernels for 0%

profile of v3, /device:TPU:57, one launch (start us, length us, event | category | flops | bytes accessed | tf_op | source)
XLA Modules:
  0.0 223.5 jit_solution(8981966127350449550)
XLA Ops:
  0.0 0.7 broadcast_add_fusion
  0.7 0.7 broadcast_subtract_fusion
  1.4 0.7 broadcast_add_fusion.1
  2.2 0.7 broadcast_subtract_fusion.1
  3.5 0.0 copy-start.6
  3.6 0.0 copy-start.7
  3.6 0.0 copy-start.5
  3.6 4.5 %fusion.58 = f32[4096,385,1]{0,1,2:T(8,128)} fusion(f32[4096]{0:T(1024)} %param.13, s32[4096]{0:T(1024)S(1)} %broadcast_add_fusion, f32[4096]{0:T(1024)S(1)} %broadcast_subtract_fusion, s32[4096]{0:T(1024)} %param.11), kind=kLoop, calls=%fused_computation.10.clone.2 | loop fusion | flops 7884800 | bytes 6373376 | tf_op jit(solution)/shard_map/krl,kc->rlc/dot_general | solution.py:237
  8.1 0.0 copy-done.6
  8.1 0.0 copy-done.7
  8.1 1.5 select_add_fusion
  9.6 0.0 copy-done.5
  9.6 29.1 %fusion = f32[97,16,385]{2,1,0:T(8,128)S(1)} fusion(f32[4096,16]{0,1:T(8,128)S(1)} %select_bitcast_fusion, f32[4096,97]{0,1:T(8,128)} %select_add_fusion, f32[4096,385,1]{0,1,2:T(8,128)} %fusion.58), kind=kOutput, calls=%fused_computation | convolution fusion | flops 14691008512 | bytes 10549312 | tf_op jit(solution)/shard_map/krl,kc->rlc/dot_general | solution.py:237
  38.7 0.0 copy-start.2
  38.7 0.0 copy-start.10
  38.7 0.0 copy-start.11
  38.7 1.5 fusion.51
  40.2 1.6 copy.38
  41.8 3.7 %collective-permute-start = (f32[97,16]{0,1:T(8,128)S(1)}, f32[97,16]{0,1:T(8,128)S(1)}, u32[]{:S(2)}, u32[]{:S(2)}) collective-permute-start(f32[97,16]{0,1:T(8,128)S(1)} %bitcast.51), channel_id=1, source_target_pairs={{15,0},{0,1},{1,2},{2,3},{3,4},{4,5},{5,6},{6,7},{7,8},{8,9},{9,10... | collective-permute-start | bytes 18632 | tf_op jit(solution)/shard_map/ppermute | solution.py:16
  45.5 0.7 abs_compare_fusion.1
  46.2 0.7 abs_compare_fusion
  46.9 0.0 copy-done.10
  46.9 0.0 copy-done.11
  46.9 0.6 multiply_multiply_fusion.1
  47.5 0.8 fusion.44
  48.3 0.0 copy-done.2
  48.3 0.0 copy-start.3
  48.3 2.6 %slice.36 = f32[97,16,383]{2,1,0:T(8,128)S(1)} slice(f32[97,16,385]{2,1,0:T(8,128)} %copy-done.2), slice={[0:97], [0:16], [1:384]} | slice | bytes 4755328 | tf_op jit(solution)/shard_map/slice | solution.py:242
  50.9 0.0 copy-done.3
  50.9 0.4 copy.37
  51.3 0.0 collective-permute-done
  51.3 0.5 copy.39
  51.8 0.0 copy-start.4
  51.8 0.1 maximum_bitcast_fusion
  51.9 5.1 %collective-permute-start.1 = (f32[16,384]{1,0:T(8,128)S(1)}, f32[16,384]{1,0:T(8,128)S(1)}, u32[]{:S(2)}, u32[]{:S(2)}) collective-permute-start(f32[16,384]{1,0:T(8,128)S(1)} %maximum_bitcast_fusion), channel_id=1, source_target_pairs={{0,16},{16,32},{32,48},{48,64},{64,80},{80,96},{96,112},{112,128},... | collective-permute-start | bytes 73736 | tf_op jit(solution)/shard_map/ppermute | solution.py:22
  57.0 0.7 sqrt.14
  57.7 0.6 sqrt.15
  58.3 0.0 collective-permute-done.1
  58.3 0.1 fusion.46
  58.4 0.0 copy-done.4
  58.4 2.2 fusion.27.x_ref
  60.6 123.3 %shard_map.91 = (f32[128,16,384]{2,1,0:T(8,128)}, f32[128,16,384]{2,1,0:T(8,128)}, f32[4,96,8,384]{3,2,1,0:T(8,128)}) custom-call(f32[96,16,384]{2,1,0:T(8,128)} %fusion.27.x_ref), custom_call_target="tpu_custom_call" | custom-call | tf_op jit(solution)/shard_map/pallas_call | solution.py:168
  183.9 0.0 copy-start.1
  183.9 3.4 %broadcast_select_fusion = (f32[128,16,384]{2,1,0:T(8,128)S(1)}, f32[128,16,384]{2,1,0:T(8,128)S(1)}) fusion(f32[128,16,384]{2,1,0:T(8,128)} %get-tuple-element.10, pred[128]{0:T(512)(128)(4,1)S(1)} %compare_select_fusion, f32[128,16,384]{2,1,0:T(8,128)} %get-tuple-element.9, pred[128]{0:T(512)(128)(4,1)S(1)} %compare_select_fusion.1), kind=kLoop, calls=%fused_computation.46 | loop fusion | flops 1572864 | bytes 12583168 | tf_op jit(solution)/shard_map/jit(_where)/select_n | solution.py:179
  187.3 0.1 copy-done.1
  187.4 0.0 copy-start.9
  187.4 0.0 copy-start.12
  187.4 0.6 pad_maximum_fusion
  188.0 0.2 copy-done.9
  188.2 0.0 copy-done.12
  188.2 6.1 %fusion.4 = f32[16,384,96]{1,2,0:T(8,128)S(1)} fusion(f32[352,16,384]{2,1,0:T(8,128)S(1)} %pad_maximum_fusion, f32[16]{0:T(128)S(1)} %sqrt.14, f32[16]{0:T(128)S(1)} %copy-done.12, f32[96,352]{1,0:T(8,128)S(1)} %multiply_negate_fusion.1, pred[96,352]{1,0:T(8,128)(4,1)S(1)} %copy-done.9), kind=kOutput, calls=%fused_computation.5 | convolution fusion | flops 1247330304 | bytes 11179136 | tf_op jit(solution)/shard_map/lip,plc->ilc/dot_general | solution.py:250
  194.3 2.8 %copy.53 = f32[16,384,96]{1,0,2:T(8,128)} copy(f32[16,384,96]{1,2,0:T(8,128)S(1)} %fusion.4) | data formatting | bytes 4718592 | tf_op jit(solution)/shard_map/lip,plc->ilc/dot_general | solution.py:250
  197.1 0.0 copy-start
  197.1 13.7 %shard_map.92 = (f32[96,16,128]{2,1,0:T(8,128)}, f32[96,16,128]{2,1,0:T(8,128)}) custom-call(f32[96,16,384]{2,1,0:T(8,128)} %bitcast.48), custom_call_target="tpu_custom_call" | custom-call | tf_op jit(solution)/shard_map/pallas_call | solution.py:215
  210.8 0.0 copy-done
  210.8 1.7 fusion.25
  212.5 0.0 copy-start.8
  212.5 0.5 pad_maximum_fusion.1
  213.0 0.3 copy-done.8
  213.3 5.9 %fusion.28 = f32[96,16,3,128]{3,0,2,1:T(8,128)S(1)} fusion(f32[96,16,3,384]{3,1,0,2:T(8,128)S(1)} %pad_maximum_fusion.1, f32[16]{0:T(128)S(1)} %sqrt.15, f32[16]{0:T(128)S(1)} %get-tuple-element.21, f32[128,384]{1,0:T(8,128)S(1)} %multiply_negate_fusion, pred[128,384]{1,0:T(8,128)(4,1)S(1)} %copy-done.8), kind=kOutput, calls=%fused_computation.41 | convolution fusion | flops 1361313792 | bytes 9683072 | tf_op jit(solution)/shard_map/lip,rlbp->rlbi/dot_general | solution.py:261
  219.3 1.6 copy.43
  220.9 2.6 %reshape.226 = f32[96,16,384]{2,1,0:T(8,128)} reshape(f32[96,16,3,128]{3,2,1,0:T(4,128)S(1)} %copy.43) | data formatting | bytes 4718592 | tf_op jit(solution)/shard_map/reshape | solution.py:262
  (11 shorter events, 0.1 us)
Async XLA Ops:
  3.5 4.6 %copy-start.6 = (f32[4096]{0:T(1024)S(1)}, f32[4096]{0:T(1024)}, u32[]{:S(2)}) copy-start(f32[4096]{0:T(1024)} %param.12) | copy-start | bytes 49156
  3.6 4.5 %copy-start.7 = (s32[4096]{0:T(1024)S(1)}, s32[4096]{0:T(1024)}, u32[]{:S(2)}) copy-start(s32[4096]{0:T(1024)} %param.10) | copy-start | bytes 49156
  3.6 6.0 %copy-start.5 = (f32[16,4096]{1,0:T(8,128)S(1)}, f32[16,4096]{1,0:T(8,128)}, u32[]{:S(2)}) copy-start(f32[16,4096]{1,0:T(8,128)} %param.9) | copy-start | bytes 786436
  38.7 9.6 %copy-start.2 = (f32[97,16,385]{2,1,0:T(8,128)}, f32[97,16,385]{2,1,0:T(8,128)S(1)}, u32[]{:S(2)}) copy-start(f32[97,16,385]{2,1,0:T(8,128)S(1)} %fusion) | copy-start | bytes 7170244
  38.7 8.2 %copy-start.10 = (f32[16]{0:T(128)S(1)}, f32[16]{0:T(128)}, u32[]{:S(2)}) copy-start(f32[16]{0:T(128)} %param.17) | copy-start | bytes 196
  38.7 8.2 %copy-start.11 = (f32[16]{0:T(128)S(1)}, f32[16]{0:T(128)}, u32[]{:S(2)}) copy-start(f32[16]{0:T(128)} %param.16) | copy-start | bytes 196
  41.8 9.5 %collective-permute-start = (f32[97,16]{0,1:T(8,128)S(1)}, f32[97,16]{0,1:T(8,128)S(1)}, u32[]{:S(2)}, u32[]{:S(2)}) collective-permute-start(f32[97,16]{0,1:T(8,128)S(1)} %bitcast.51), channel_id=1, source_target_pairs={{15,0},{0,1},{1,2},{2,3},{3,4},{4,5},{5,6},{6,7},{7,8},{8,9},{9,10... | collective-permute-start | bytes 18632 | tf_op jit(solution)/shard_map/ppermute | solution.py:16
  48.3 2.7 %copy-start.3 = (f32[97,16,1]{2,1,0:T(8,128)S(1)}, f32[97,16,1]{2,1,0:T(8,128)}, u32[]{:S(2)}) copy-start(f32[97,16,1]{2,1,0:T(8,128)} %get-tuple-element.15) | copy-start | bytes 18628
  51.8 6.6 %copy-start.4 = (f32[96,16,384]{2,1,0:T(8,128)S(1)}, f32[96,16,384]{2,1,0:T(8,128)}, u32[]{:S(2)}) copy-start(f32[96,16,384]{2,1,0:T(8,128)} %param.15) | copy-start | bytes 7077892
  51.9 6.4 %collective-permute-start.1 = (f32[16,384]{1,0:T(8,128)S(1)}, f32[16,384]{1,0:T(8,128)S(1)}, u32[]{:S(2)}, u32[]{:S(2)}) collective-permute-start(f32[16,384]{1,0:T(8,128)S(1)} %maximum_bitcast_fusion), channel_id=1, source_target_pairs={{0,16},{16,32},{32,48},{48,64},{64,80},{80,96},{96,112},{112,128},... | collective-permute-start | bytes 73736 | tf_op jit(solution)/shard_map/ppermute | solution.py:22
  183.9 3.5 %copy-start.1 = (f32[96,16,384]{2,1,0:T(8,128)S(1)}, f32[96,16,384]{2,1,0:T(8,128)}, u32[]{:S(2)}) copy-start(f32[96,16,384]{2,1,0:T(8,128)} %fusion.27.x_ref) | copy-start | bytes 7077892
  187.4 0.8 copy-start.9
  187.4 0.8 copy-start.12
  197.1 13.7 %copy-start = (f32[16,384,96]{1,0,2:T(8,128)S(1)}, f32[16,384,96]{1,0,2:T(8,128)}, u32[]{:S(2)}) copy-start(f32[16,384,96]{1,0,2:T(8,128)} %copy.53) | copy-start | bytes 7077892
  212.5 0.8 copy-start.8

commit v4 on v2

--- a/solution.py
+++ b/solution.py
@@ -190,9 +190,9 @@
     values_t = jnp.where(live_slot[:, None], jnp.transpose(obs_values), 0.0)
     row_w = corner_weights(obs_rows, row_frac, tile_rows + 1)
     col_w = corner_weights(obs_cols, col_frac, tile_cols + 1)
-    row_values = row_w[:, :, None] * values_t[:, None, :]
+    row_values = values_t[:, :, None] * row_w[:, None, :]
     extended = jnp.einsum(
-        "krl,kc->rlc", row_values, col_w, precision=lax.Precision.HIGH
+        "klr,kc->rlc", row_values, col_w, precision=lax.Precision.HIGH
     )
     edge_column = from_behind(extended[:, :, tile_cols], "lon", 1)
     folded = jnp.concatenate(

time: 218 us -> 212 us (0.972)
  matrix products: 38.6 us -> 32.4 us
  other arithmetic: 15.9 us -> 11.9 us
  local copies, waits for them, and re-layouts: 11.1 us -> 15 us
    dot_general x1, matrix products: 29.1 us -> 22.9 us  [shards(): jnp.einsum('klr,kc->rlc', row_values, col_w, precision=lax.Precision.HIGH)]
    dot_general x1 -> x0, other arithmetic: 4.51 us -> none  [shards(): jnp.einsum('krl,kc->rlc', row_values, col_w, precision=lax.Precision.HIGH)]
    dot_general x0 -> x1, local copies, waits for them, and re-layouts: none -> 3.9 us  [shards(): jnp.einsum('klr,kc->rlc', row_values, col_w, precision=lax.Precision.HIGH)]
where the time goes in v4:
time: 212 us; the launch traced here: 211 us
  Pallas kernels  122 us (58%)
  matrix products  32.4 us (15%)
  starting transfers between devices  16.8 us (8%)
  local copies, waits for them, and re-layouts  15 us (7%)
  other arithmetic  11.9 us (6%)
  waiting for transfers between devices  11.7 us (6%)
    pallas_call x1, Pallas kernels, lat_halo_kernel(): pl.pallas_call(functools.partial(relay_halo_body, count, span, rows, far)...  122 us
    dot_general x1, matrix products, shards(): jnp.einsum('klr,kc->rlc', row_values, col_w, precision=lax.Precision.HIGH)  22.9 us
    ppermute x1, waiting for transfers between devices, with_halo(): lax.ppermute(lax.slice_in_dim(block, block.shape[dim] - width, None, axis...  6.59 us
    dot_general x1, matrix products, shards(): jnp.einsum('lip,plc->ilc', lat_kernel, window, precision=lax.Precision.HIGH)  6.07 us
    ppermute x1, starting transfers between devices, with_halo(): lax.ppermute(lax.slice_in_dim(block, block.shape[dim] - width, None, axis...  5.64 us
    ppermute x1, starting transfers between devices, shifted(): return lax.ppermute(block, axis, route)  5.36 us
    ppermute x1, waiting for transfers between devices, with_halo(): lax.ppermute(lax.slice_in_dim(block, 0, width, axis=dim), axis, backward)  4.4 us
  transfers between devices with their start and end apart: 4, of which 3 were waited for; matrix products, arithmetic and copies ran while one was open for 2% of the time, Pallas kernels for 0%

profile of v4, /device:TPU:57, one launch (start us, length us, event | category | flops | bytes accessed | tf_op | source)
XLA Modules:
  0.0 211.3 jit_solution(17279352344710015689)
XLA Ops:
  0.0 0.0 copy-start.5
  0.0 0.0 copy-start.4
  0.0 0.7 broadcast_add_fusion
  0.7 0.7 broadcast_subtract_fusion
  2.1 0.7 broadcast_add_fusion.1
  2.8 0.7 broadcast_subtract_fusion.1
  3.6 1.0 select_add_fusion
  4.6 1.0 select_bitcast_fusion
  5.6 0.0 copy-done.5
  5.6 0.0 copy-done.4
  5.6 22.9 %fusion = f32[385,16,97]{2,0,1:T(8,128)} fusion(f32[4096,97]{0,1:T(8,128)S(1)} %select_add_fusion, f32[4096,16]{0,1:T(8,128)S(1)} %select_bitcast_fusion, f32[4096]{0:T(1024)S(1)} %copy-done.4, s32[4096]{0:T(1024)S(1)} %broadcast_add_fusion.1, f32[4096]{0:T(1024)S(1)} %broadcast_subtract_fusion.1, s32[4096]{0:T(1024)S(1)} %copy-done.5), kind=kOutput, calls=%fused_computation | convolution fusion | flops 14698893312 | bytes 4307008 | tf_op jit(solution)/shard_map/klr,kc->rlc/dot_general | solution.py:194
  28.5 3.9 %copy.37 = f32[385,16,97]{0,1,2:T(8,128)S(1)} copy(f32[385,16,97]{2,0,1:T(8,128)} %fusion) | data formatting | bytes 4780160 | tf_op jit(solution)/shard_map/klr,kc->rlc/dot_general | solution.py:194
  32.4 0.0 copy-start.1
  32.4 0.0 copy-start.6
  32.4 0.0 copy-start.7
  32.4 1.4 fusion.51
  33.8 1.6 copy.39
  35.5 3.7 %collective-permute-start = (f32[97,16]{0,1:T(8,128)S(1)}, f32[97,16]{0,1:T(8,128)S(1)}, u32[]{:S(2)}, u32[]{:S(2)}) collective-permute-start(f32[97,16]{0,1:T(8,128)S(1)} %bitcast.46), channel_id=1, source_target_pairs={{15,0},{0,1},{1,2},{2,3},{3,4},{4,5},{5,6},{6,7},{7,8},{8,9},{9,10... | collective-permute-start | bytes 18632 | tf_op jit(solution)/shard_map/ppermute | solution.py:16
  39.2 0.0 copy-done.6
  39.3 0.0 copy-done.7
  39.3 0.2 fusion.44
  39.5 0.0 copy-done.1
  39.5 0.0 copy-start.2
  39.5 2.6 %slice.44 = f32[97,16,383]{2,1,0:T(8,128)S(1)} slice(f32[97,16,385]{2,1,0:T(8,128)} %bitcast.42), slice={[0:97], [0:16], [1:384]} | slice | bytes 4755328 | tf_op jit(solution)/shard_map/slice | solution.py:199
  42.2 0.0 copy-done.2
  42.2 0.4 copy.38
  42.6 0.0 collective-permute-done
  42.6 0.5 copy.40
  43.0 0.1 maximum_bitcast_fusion
  43.1 0.0 copy-start.3
  43.1 5.4 %collective-permute-start.1 = (f32[16,384]{1,0:T(8,128)S(1)}, f32[16,384]{1,0:T(8,128)S(1)}, u32[]{:S(2)}, u32[]{:S(2)}) collective-permute-start(f32[16,384]{1,0:T(8,128)S(1)} %maximum_bitcast_fusion), channel_id=1, source_target_pairs={{0,16},{16,32},{32,48},{48,64},{64,80},{80,96},{96,112},{112,128},... | collective-permute-start | bytes 73736 | tf_op jit(solution)/shard_map/ppermute | solution.py:22
  48.5 0.7 collective-permute-done.1
  49.2 0.1 fusion.46
  49.3 0.0 copy-done.3
  49.3 2.2 %fusion.27.x_ref = f32[96,16,384]{2,1,0:T(8,128)} fusion(f32[96,16,384]{2,1,0:T(8,128)S(1)} %copy-done.3, f32[97,16,383]{2,1,0:T(8,128)S(1)} %slice.44, f32[97,16,1]{2,1,0:T(8,128)S(1)} %copy.40, f32[1,16,384]{2,1,0:T(8,128)S(1)} %fusion.46), kind=kLoop, calls=%fused_computation.34 | loop fusion | flops 3538944 | bytes 7127040 | tf_op jit(solution)/shard_map/mul | solution.py:203
  51.4 122.5 %shard_map.91 = (f32[128,16,384]{2,1,0:T(8,128)}, f32[128,16,384]{2,1,0:T(8,128)}, f32[4,96,8,384]{3,2,1,0:T(8,128)}) custom-call(f32[96,16,384]{2,1,0:T(8,128)} %fusion.27.x_ref), custom_call_target="tpu_custom_call" | custom-call | tf_op jit(solution)/shard_map/pallas_call | solution.py:168
  173.9 0.0 copy-start
  173.9 3.4 %broadcast_select_fusion = (f32[128,16,384]{2,1,0:T(8,128)S(1)}, f32[128,16,384]{2,1,0:T(8,128)S(1)}) fusion(f32[128,16,384]{2,1,0:T(8,128)} %get-tuple-element.8, pred[128]{0:T(512)(128)(4,1)S(1)} %compare_select_fusion, f32[128,16,384]{2,1,0:T(8,128)} %get-tuple-element.7, pred[128]{0:T(512)(128)(4,1)S(1)} %compare_select_fusion.1), kind=kLoop, calls=%fused_computation.44 | loop fusion | flops 1572864 | bytes 12583168 | tf_op jit(solution)/shard_map/jit(_where)/select_n | solution.py:179
  177.3 0.1 copy-done
  177.5 0.6 pad_maximum_fusion
  178.1 6.1 %fusion.4 = f32[16,384,96]{1,2,0:T(8,128)S(1)} fusion(f32[352,16,384]{2,1,0:T(8,128)S(1)} %pad_maximum_fusion, f32[16]{0:T(128)S(1)} %sqrt.14, f32[16]{0:T(128)S(1)} %get-tuple-element.19, f32[96,352]{1,0:T(8,128)S(1)} %multiply_negate_fusion.1, pred[96,352]{1,0:T(8,128)(4,1)S(1)} %abs_compare_fusion.1), kind=kOutput, calls=%fused_computation.5 | convolution fusion | flops 1247330304 | bytes 11179136 | tf_op jit(solution)/shard_map/lip,plc->ilc/dot_general | solution.py:207
  184.1 0.2 fusion.52
  184.3 5.6 %collective-permute-start.2 = (f32[96,16,128]{2,0,1:T(8,128)S(1)}, f32[96,16,128]{2,0,1:T(8,128)S(1)}, u32[]{:S(2)}, u32[]{:S(2)}) collective-permute-start(f32[96,16,128]{2,0,1:T(8,128)S(1)} %get-tuple-element.15), channel_id=1, source_target_pairs={{0,1},{1,2},{2,3},{3,4},{4,5},{5,6},{6,7},{7,8},{8,9},{9,10},{10,1... | collective-permute-start | bytes 2359304 | tf_op jit(solution)/shard_map/ppermute | solution.py:31
  190.0 2.2 %collective-permute-start.3 = (f32[96,16,128]{2,0,1:T(8,128)S(1)}, f32[96,16,128]{2,0,1:T(8,128)S(1)}, u32[]{:S(2)}, u32[]{:S(2)}) collective-permute-start(f32[96,16,128]{2,0,1:T(8,128)S(1)} %get-tuple-element.16), channel_id=1, source_target_pairs={{1,0},{2,1},{3,2},{4,3},{5,4},{6,5},{7,6},{8,7},{9,8},{10,9},{11,1... | collective-permute-start | bytes 2359304 | tf_op jit(solution)/shard_map/ppermute | solution.py:34
  192.2 0.1 abs_compare_fusion
  192.3 6.6 %collective-permute-done.2 = f32[96,16,128]{2,0,1:T(8,128)S(1)} collective-permute-done((f32[96,16,128]{2,0,1:T(8,128)S(1)}, f32[96,16,128]{2,0,1:T(8,128)S(1)}, u32[]{:S(2)}, u32[]{:S(2)}) %collective-permute-start.2) | collective-permute-done | bytes 786464 | tf_op jit(solution)/shard_map/ppermute | solution.py:31
  198.9 4.4 %collective-permute-done.3 = f32[96,16,128]{2,0,1:T(8,128)S(1)} collective-permute-done((f32[96,16,128]{2,0,1:T(8,128)S(1)}, f32[96,16,128]{2,0,1:T(8,128)S(1)}, u32[]{:S(2)}, u32[]{:S(2)}) %collective-permute-start.3) | collective-permute-done | bytes 786464 | tf_op jit(solution)/shard_map/ppermute | solution.py:34
  203.3 0.4 fusion.25
  203.6 3.5 %fusion.28 = f32[96,16,3,128]{3,0,2,1:T(8,128)S(1)} fusion(f32[16]{0:T(128)S(1)} %sqrt.15, f32[16]{0:T(128)S(1)} %get-tuple-element.17, f32[128,384]{1,0:T(8,128)S(1)} %multiply_negate_fusion, pred[128,384]{1,0:T(8,128)(4,1)S(1)} %abs_compare_fusion, f32[96,16,1,384]{3,0,1,2:T(8,128)S(1)} %get-tuple-element.14, f32[96,16,1,384]{3,0,1,2:T(8,128)S(1)} %bitcast.45, ...), kind=kOutput, calls=%fused_computation.39 | convolution fusion | flops 1364852736 | bytes 9683072 | tf_op jit(solution)/shard_map/lip,rlbp->rlbi/dot_general | solution.py:218
  207.1 1.6 copy.43
  208.7 2.6 %reshape.210 = f32[96,16,384]{2,1,0:T(8,128)} reshape(f32[96,16,3,128]{3,2,1,0:T(4,128)S(1)} %copy.43) | data formatting | bytes 4718592 | tf_op jit(solution)/shard_map/reshape | solution.py:219
  (14 shorter events, 0.2 us)
Async XLA Ops:
  0.0 5.6 %copy-start.5 = (s32[4096]{0:T(1024)S(1)}, s32[4096]{0:T(1024)}, u32[]{:S(2)}) copy-start(s32[4096]{0:T(1024)} %param.11) | copy-start | bytes 49156
  0.0 5.6 %copy-start.4 = (f32[4096]{0:T(1024)S(1)}, f32[4096]{0:T(1024)}, u32[]{:S(2)}) copy-start(f32[4096]{0:T(1024)} %param.13) | copy-start | bytes 49156
  32.4 7.1 %copy-start.1 = (f32[385,16,97]{0,1,2:T(8,128)}, f32[385,16,97]{0,1,2:T(8,128)S(1)}, u32[]{:S(2)}) copy-start(f32[385,16,97]{0,1,2:T(8,128)S(1)} %copy.37) | copy-start | bytes 7170244
  32.4 6.9 %copy-start.6 = (f32[16]{0:T(128)S(1)}, f32[16]{0:T(128)}, u32[]{:S(2)}) copy-start(f32[16]{0:T(128)} %param.17) | copy-start | bytes 196
  32.4 6.9 %copy-start.7 = (f32[16]{0:T(128)S(1)}, f32[16]{0:T(128)}, u32[]{:S(2)}) copy-start(f32[16]{0:T(128)} %param.16) | copy-start | bytes 196
  35.5 7.1 %collective-permute-start = (f32[97,16]{0,1:T(8,128)S(1)}, f32[97,16]{0,1:T(8,128)S(1)}, u32[]{:S(2)}, u32[]{:S(2)}) collective-permute-start(f32[97,16]{0,1:T(8,128)S(1)} %bitcast.46), channel_id=1, source_target_pairs={{15,0},{0,1},{1,2},{2,3},{3,4},{4,5},{5,6},{6,7},{7,8},{8,9},{9,10... | collective-permute-start | bytes 18632 | tf_op jit(solution)/shard_map/ppermute | solution.py:16
  39.5 2.7 %copy-start.2 = (f32[97,16,1]{2,1,0:T(8,128)S(1)}, f32[97,16,1]{2,1,0:T(8,128)}, u32[]{:S(2)}) copy-start(f32[97,16,1]{2,1,0:T(8,128)} %get-tuple-element.11) | copy-start | bytes 18628
  43.1 6.2 %copy-start.3 = (f32[96,16,384]{2,1,0:T(8,128)S(1)}, f32[96,16,384]{2,1,0:T(8,128)}, u32[]{:S(2)}) copy-start(f32[96,16,384]{2,1,0:T(8,128)} %param.15) | copy-start | bytes 7077892
  43.1 6.1 %collective-permute-start.1 = (f32[16,384]{1,0:T(8,128)S(1)}, f32[16,384]{1,0:T(8,128)S(1)}, u32[]{:S(2)}, u32[]{:S(2)}) collective-permute-start(f32[16,384]{1,0:T(8,128)S(1)} %maximum_bitcast_fusion), channel_id=1, source_target_pairs={{0,16},{16,32},{32,48},{48,64},{64,80},{80,96},{96,112},{112,128},... | collective-permute-start | bytes 73736 | tf_op jit(solution)/shard_map/ppermute | solution.py:22
  173.9 3.5 %copy-start = (f32[96,16,384]{2,1,0:T(8,128)S(1)}, f32[96,16,384]{2,1,0:T(8,128)}, u32[]{:S(2)}) copy-start(f32[96,16,384]{2,1,0:T(8,128)} %fusion.27.x_ref) | copy-start | bytes 7077892
  184.3 14.6 %collective-permute-start.2 = (f32[96,16,128]{2,0,1:T(8,128)S(1)}, f32[96,16,128]{2,0,1:T(8,128)S(1)}, u32[]{:S(2)}, u32[]{:S(2)}) collective-permute-start(f32[96,16,128]{2,0,1:T(8,128)S(1)} %get-tuple-element.15), channel_id=1, source_target_pairs={{0,1},{1,2},{2,3},{3,4},{4,5},{5,6},{6,7},{7,8},{8,9},{9,10},{10,1... | collective-permute-start | bytes 2359304 | tf_op jit(solution)/shard_map/ppermute | solution.py:31
  190.0 13.3 %collective-permute-start.3 = (f32[96,16,128]{2,0,1:T(8,128)S(1)}, f32[96,16,128]{2,0,1:T(8,128)S(1)}, u32[]{:S(2)}, u32[]{:S(2)}) collective-permute-start(f32[96,16,128]{2,0,1:T(8,128)S(1)} %get-tuple-element.16), channel_id=1, source_target_pairs={{1,0},{2,1},{3,2},{4,3},{5,4},{6,5},{7,6},{8,7},{9,8},{10,9},{11,1... | collective-permute-start | bytes 2359304 | tf_op jit(solution)/shard_map/ppermute | solution.py:34

commit v5 on v4

--- a/solution.py
+++ b/solution.py
@@ -78,7 +78,7 @@
     return jnp.concatenate(parts, axis=0)
 
 
-def relay_halo_body(count, span, rows, far, x_ref, below_ref, above_ref, relay_ref, send_sem, recv_sem):
+def relay_halo_body(count, span, pieces, rows, far, x_ref, below_ref, above_ref, relay_ref, send_sem, recv_sem):
     here = lax.axis_index("lat")
     column = lax.axis_index("lon")
     mesh = pl.DeviceIdType.MESH
@@ -93,30 +93,34 @@
     low, high = pl.ds(0, half), pl.ds(half, half)
     near_below = below_ref.at[pl.ds(far, rows)]
     near_above = above_ref.at[pl.ds(0, rows)]
-    plan = {
-        0: (here + 2 < count, 2, x_ref.at[pl.ds(rows - far, far)], below_ref.at[pl.ds(0, far)], here >= 2),
-        1: (here >= 2, -2, x_ref.at[pl.ds(0, far)], above_ref.at[pl.ds(rows, far)], here + 2 < count),
-        2: (jnp.logical_and(up_exists, jnp.logical_not(cross_up)), 1, x_ref, near_below,
-            jnp.logical_and(down_exists, jnp.logical_not(first_of))),
-        3: (jnp.logical_and(down_exists, jnp.logical_not(first_of)), -1, x_ref, near_above,
-            jnp.logical_and(up_exists, jnp.logical_not(cross_up))),
-        4: (cross_up, span, x_ref.at[:, low], relay_ref.at[0], jnp.logical_and(last_of, here >= span)),
-        5: (cross_up, 1 - span, x_ref.at[:, high], relay_ref.at[1], jnp.logical_and(first_of, here + span < count)),
-        6: (cross_down, -span, x_ref.at[:, low], relay_ref.at[2], jnp.logical_and(first_of, here + span < count)),
-        7: (cross_down, span - 1, x_ref.at[:, high], relay_ref.at[3], jnp.logical_and(last_of, here >= span)),
-        8: (jnp.logical_and(last_of, here >= span), 1 - span, relay_ref.at[0], near_below.at[:, low],
-            jnp.logical_and(first_of, here >= span)),
-        9: (jnp.logical_and(first_of, here + span < count), span, relay_ref.at[1], near_below.at[:, high],
-            jnp.logical_and(first_of, here >= span)),
-        10: (jnp.logical_and(first_of, here + span < count), span - 1, relay_ref.at[2], near_above.at[:, low],
-             jnp.logical_and(last_of, up_exists)),
-        11: (jnp.logical_and(last_of, here >= span), -span, relay_ref.at[3], near_above.at[:, high],
-             jnp.logical_and(last_of, up_exists)),
-    }
-    feeds = {8: 4, 9: 5, 10: 6, 11: 7}
+    plan = [
+        (here + 2 < count, 2, x_ref.at[pl.ds(rows - far, far)], below_ref.at[pl.ds(0, far)], here >= 2),
+        (here >= 2, -2, x_ref.at[pl.ds(0, far)], above_ref.at[pl.ds(rows, far)], here + 2 < count),
+        (jnp.logical_and(up_exists, jnp.logical_not(cross_up)), 1, x_ref, near_below,
+         jnp.logical_and(down_exists, jnp.logical_not(first_of))),
+        (jnp.logical_and(down_exists, jnp.logical_not(first_of)), -1, x_ref, near_above,
+         jnp.logical_and(up_exists, jnp.logical_not(cross_up))),
+    ]
+    feeds = {}
+    relay_up_a = jnp.logical_and(last_of, here >= span)
+    relay_up_b = jnp.logical_and(first_of, here + span < count)
+    lands_below = jnp.logical_and(first_of, here >= span)
+    lands_above = jnp.logical_and(last_of, up_exists)
+    routes = [
+        (cross_up, span, low, 0, relay_up_a, 1 - span, near_below, lands_below),
+        (cross_up, 1 - span, high, 1, relay_up_b, span, near_below, lands_below),
+        (cross_down, -span, low, 2, relay_up_b, span - 1, near_above, lands_above),
+        (cross_down, span - 1, high, 3, relay_up_a, -span, near_above, lands_above),
+    ]
+    for start, first_hop, levels, slot, relays, second_hop, target, lands in routes:
+        for piece in range(pieces):
+            part = pl.ds(piece * (rows // pieces), rows // pieces)
+            plan.append((start, first_hop, x_ref.at[part, levels], relay_ref.at[slot, part], relays))
+            feeds[len(plan)] = len(plan) - 1
+            plan.append((relays, second_hop, relay_ref.at[slot, part], target.at[part, levels], lands))
 
     barrier = pltpu.get_barrier_semaphore()
-    offsets = sorted({offset for _, offset, _, _, _ in plan.values()})
+    offsets = sorted({entry[1] for entry in plan})
     for offset in offsets:
         neighbour = lax.rem(here + offset + count, count)
         pl.semaphore_signal(barrier, 1, device_id=(neighbour, column), device_id_type=mesh)
@@ -136,14 +140,15 @@
         def _():
             copy(slot, here + offset).start()
 
-    for slot in range(8):
-        when_start(slot)
+    for slot in range(len(plan)):
+        if slot not in feeds:
+            when_start(slot)
     for slot, source in feeds.items():
         @pl.when(plan[slot][0])
         def _():
             copy(source, here).wait_recv()
             copy(slot, here + plan[slot][1]).start()
-    for slot in range(12):
+    for slot in range(len(plan)):
         sends, offset, _, _, receives = plan[slot]
 
         @pl.when(sends)
@@ -165,12 +170,14 @@
     halo_shape = jax.ShapeDtypeStruct((width,) + block.shape[1:], block.dtype)
     levels = block.shape[1]
     relay_shape = jax.ShapeDtypeStruct((4, rows, levels // 2, block.shape[2]), block.dtype)
+    pieces = 3 if rows % 3 == 0 else 1
+    slots = 4 + 8 * pieces
     below, above, _ = pl.pallas_call(
-        functools.partial(relay_halo_body, count, span, rows, far),
+        functools.partial(relay_halo_body, count, span, pieces, rows, far),
         out_shape=(halo_shape, halo_shape, relay_shape),
         in_specs=[pl.BlockSpec(memory_space=pl.ANY)],
         out_specs=(pl.BlockSpec(memory_space=pl.ANY),) * 3,
-        scratch_shapes=[pltpu.SemaphoreType.DMA((12,)), pltpu.SemaphoreType.DMA((12,))],
+        scratch_shapes=[pltpu.SemaphoreType.DMA((slots,)), pltpu.SemaphoreType.DMA((slots,))],
         compiler_params=pltpu.CompilerParams(collective_id=0, has_side_effects=True),
     )(block)
     here = lax.axis_index("lat")

time: 212 us -> 203 us (0.958)
  the two profiles are of different devices: /device:TPU:57 before, /device:TPU:185 now
where the time goes in v5:
time: 203 us
  Pallas kernels  99.4 us (49%)
  matrix products  32.4 us (16%)
  starting transfers between devices  31 us (15%)
  local copies, waits for them, and re-layouts  15 us (7%)
  other arithmetic  11.9 us (6%)
  waiting for transfers between devices  11.9 us (6%)
    pallas_call x1, Pallas kernels, lat_halo_kernel(): pl.pallas_call(functools.partial(relay_halo_body, count, span, pieces, ro...  99.4 us
    dot_general x1, matrix products, shards(): jnp.einsum('klr,kc->rlc', row_values, col_w, precision=lax.Precision.HIGH)  22.9 us
    ppermute x1, starting transfers between devices, with_halo(): lax.ppermute(lax.slice_in_dim(block, block.shape[dim] - width, None, axis...  18.8 us
    ppermute x1, waiting for transfers between devices, with_halo(): lax.ppermute(lax.slice_in_dim(block, block.shape[dim] - width, None, axis...  6.59 us
    ppermute x1, starting transfers between devices, shifted(): return lax.ppermute(block, axis, route)  6.36 us
    dot_general x1, matrix products, shards(): jnp.einsum('lip,plc->ilc', lat_kernel, window, precision=lax.Precision.HIGH)  6.07 us
    ppermute x1, waiting for transfers between devices, with_halo(): lax.ppermute(lax.slice_in_dim(block, 0, width, axis=dim), axis, backward)  4.4 us
  transfers between devices with their start and end apart: 4, of which 3 were waited for; matrix products, arithmetic and copies ran while one was open for 2% of the time, Pallas kernels for 0%

profile of v5, /device:TPU:185, one launch (start us, length us, event | category | flops | bytes accessed | tf_op | source)
XLA Modules:
  0.0 202.6 jit_solution(14133478642568271841)
XLA Ops:
  0.0 0.0 copy-start.5
  0.0 0.0 copy-start.4
  0.0 0.7 broadcast_add_fusion
  0.7 0.7 broadcast_subtract_fusion
  2.1 0.7 broadcast_add_fusion.1
  2.8 0.7 broadcast_subtract_fusion.1
  3.6 1.0 select_add_fusion
  4.6 1.0 select_bitcast_fusion
  5.6 0.0 copy-done.5
  5.6 0.0 copy-done.4
  5.6 22.9 %fusion = f32[385,16,97]{2,0,1:T(8,128)} fusion(f32[4096,97]{0,1:T(8,128)S(1)} %select_add_fusion, f32[4096,16]{0,1:T(8,128)S(1)} %select_bitcast_fusion, f32[4096]{0:T(1024)S(1)} %copy-done.4, s32[4096]{0:T(1024)S(1)} %broadcast_add_fusion.1, f32[4096]{0:T(1024)S(1)} %broadcast_subtract_fusion.1, s32[4096]{0:T(1024)S(1)} %copy-done.5), kind=kOutput, calls=%fused_computation | convolution fusion | flops 14698893312 | bytes 4307008 | tf_op jit(solution)/shard_map/klr,kc->rlc/dot_general | solution.py:201
  28.5 3.9 %copy.37 = f32[385,16,97]{0,1,2:T(8,128)S(1)} copy(f32[385,16,97]{2,0,1:T(8,128)} %fusion) | data formatting | bytes 4780160 | tf_op jit(solution)/shard_map/klr,kc->rlc/dot_general | solution.py:201
  32.4 0.0 copy-start.1
  32.4 0.0 copy-start.6
  32.4 0.0 copy-start.7
  32.4 1.4 fusion.51
  33.8 1.6 copy.39
  35.5 3.7 %collective-permute-start = (f32[97,16]{0,1:T(8,128)S(1)}, f32[97,16]{0,1:T(8,128)S(1)}, u32[]{:S(2)}, u32[]{:S(2)}) collective-permute-start(f32[97,16]{0,1:T(8,128)S(1)} %bitcast.46), channel_id=1, source_target_pairs={{15,0},{0,1},{1,2},{2,3},{3,4},{4,5},{5,6},{6,7},{7,8},{8,9},{9,10... | collective-permute-start | bytes 18632 | tf_op jit(solution)/shard_map/ppermute | solution.py:16
  39.2 0.0 copy-done.6
  39.3 0.0 copy-done.7
  39.3 0.2 fusion.44
  39.5 0.0 copy-done.1
  39.5 0.0 copy-start.2
  39.5 2.6 %slice.44 = f32[97,16,383]{2,1,0:T(8,128)S(1)} slice(f32[97,16,385]{2,1,0:T(8,128)} %bitcast.42), slice={[0:97], [0:16], [1:384]} | slice | bytes 4755328 | tf_op jit(solution)/shard_map/slice | solution.py:206
  42.2 0.0 copy-done.2
  42.2 0.4 copy.38
  42.6 0.0 collective-permute-done
  42.6 0.5 copy.40
  43.0 0.1 maximum_bitcast_fusion
  43.1 0.0 copy-start.3
  43.1 6.4 %collective-permute-start.1 = (f32[16,384]{1,0:T(8,128)S(1)}, f32[16,384]{1,0:T(8,128)S(1)}, u32[]{:S(2)}, u32[]{:S(2)}) collective-permute-start(f32[16,384]{1,0:T(8,128)S(1)} %maximum_bitcast_fusion), channel_id=1, source_target_pairs={{0,16},{16,32},{32,48},{48,64},{64,80},{80,96},{96,112},{112,128},... | collective-permute-start | bytes 73736 | tf_op jit(solution)/shard_map/ppermute | solution.py:22
  49.5 0.9 collective-permute-done.1
  50.4 0.1 fusion.46
  50.5 0.0 copy-done.3
  50.5 2.2 %fusion.27.x_ref = f32[96,16,384]{2,1,0:T(8,128)} fusion(f32[96,16,384]{2,1,0:T(8,128)S(1)} %copy-done.3, f32[97,16,383]{2,1,0:T(8,128)S(1)} %slice.44, f32[97,16,1]{2,1,0:T(8,128)S(1)} %copy.40, f32[1,16,384]{2,1,0:T(8,128)S(1)} %fusion.46), kind=kLoop, calls=%fused_computation.34 | loop fusion | flops 3538944 | bytes 7127040 | tf_op jit(solution)/shard_map/mul | solution.py:210
  52.7 99.4 %shard_map.91 = (f32[128,16,384]{2,1,0:T(8,128)}, f32[128,16,384]{2,1,0:T(8,128)}, f32[4,96,8,384]{3,2,1,0:T(8,128)}) custom-call(f32[96,16,384]{2,1,0:T(8,128)} %fusion.27.x_ref), custom_call_target="tpu_custom_call" | custom-call | tf_op jit(solution)/shard_map/pallas_call | solution.py:175
  152.1 0.0 copy-start
  152.1 3.4 %broadcast_select_fusion = (f32[128,16,384]{2,1,0:T(8,128)S(1)}, f32[128,16,384]{2,1,0:T(8,128)S(1)}) fusion(f32[128,16,384]{2,1,0:T(8,128)} %get-tuple-element.8, pred[128]{0:T(512)(128)(4,1)S(1)} %compare_select_fusion, f32[128,16,384]{2,1,0:T(8,128)} %get-tuple-element.7, pred[128]{0:T(512)(128)(4,1)S(1)} %compare_select_fusion.1), kind=kLoop, calls=%fused_computation.44 | loop fusion | flops 1572864 | bytes 12583168 | tf_op jit(solution)/shard_map/jit(_where)/select_n | solution.py:186
  155.5 0.1 copy-done
  155.6 0.6 pad_maximum_fusion
  156.2 6.1 %fusion.4 = f32[16,384,96]{1,2,0:T(8,128)S(1)} fusion(f32[352,16,384]{2,1,0:T(8,128)S(1)} %pad_maximum_fusion, f32[16]{0:T(128)S(1)} %sqrt.14, f32[16]{0:T(128)S(1)} %get-tuple-element.19, f32[96,352]{1,0:T(8,128)S(1)} %multiply_negate_fusion.1, pred[96,352]{1,0:T(8,128)(4,1)S(1)} %abs_compare_fusion.1), kind=kOutput, calls=%fused_computation.5 | convolution fusion | flops 1247330304 | bytes 11179136 | tf_op jit(solution)/shard_map/lip,plc->ilc/dot_general | solution.py:214
  162.3 0.2 fusion.52
  162.4 18.8 %collective-permute-start.2 = (f32[96,16,128]{2,0,1:T(8,128)S(1)}, f32[96,16,128]{2,0,1:T(8,128)S(1)}, u32[]{:S(2)}, u32[]{:S(2)}) collective-permute-start(f32[96,16,128]{2,0,1:T(8,128)S(1)} %get-tuple-element.15), channel_id=1, source_target_pairs={{0,1},{1,2},{2,3},{3,4},{4,5},{5,6},{6,7},{7,8},{8,9},{9,10},{10,1... | collective-permute-start | bytes 2359304 | tf_op jit(solution)/shard_map/ppermute | solution.py:31
  181.2 2.2 %collective-permute-start.3 = (f32[96,16,128]{2,0,1:T(8,128)S(1)}, f32[96,16,128]{2,0,1:T(8,128)S(1)}, u32[]{:S(2)}, u32[]{:S(2)}) collective-permute-start(f32[96,16,128]{2,0,1:T(8,128)S(1)} %get-tuple-element.16), channel_id=1, source_target_pairs={{1,0},{2,1},{3,2},{4,3},{5,4},{6,5},{7,6},{8,7},{9,8},{10,9},{11,1... | collective-permute-start | bytes 2359304 | tf_op jit(solution)/shard_map/ppermute | solution.py:34
  183.4 0.1 abs_compare_fusion
  183.5 6.6 %collective-permute-done.2 = f32[96,16,128]{2,0,1:T(8,128)S(1)} collective-permute-done((f32[96,16,128]{2,0,1:T(8,128)S(1)}, f32[96,16,128]{2,0,1:T(8,128)S(1)}, u32[]{:S(2)}, u32[]{:S(2)}) %collective-permute-start.2) | collective-permute-done | bytes 786464 | tf_op jit(solution)/shard_map/ppermute | solution.py:31
  190.1 4.4 %collective-permute-done.3 = f32[96,16,128]{2,0,1:T(8,128)S(1)} collective-permute-done((f32[96,16,128]{2,0,1:T(8,128)S(1)}, f32[96,16,128]{2,0,1:T(8,128)S(1)}, u32[]{:S(2)}, u32[]{:S(2)}) %collective-permute-start.3) | collective-permute-done | bytes 786464 | tf_op jit(solution)/shard_map/ppermute | solution.py:34
  194.5 0.4 fusion.25
  194.9 3.5 %fusion.28 = f32[96,16,3,128]{3,0,2,1:T(8,128)S(1)} fusion(f32[16]{0:T(128)S(1)} %sqrt.15, f32[16]{0:T(128)S(1)} %get-tuple-element.17, f32[128,384]{1,0:T(8,128)S(1)} %multiply_negate_fusion, pred[128,384]{1,0:T(8,128)(4,1)S(1)} %abs_compare_fusion, f32[96,16,1,384]{3,0,1,2:T(8,128)S(1)} %get-tuple-element.14, f32[96,16,1,384]{3,0,1,2:T(8,128)S(1)} %bitcast.45, ...), kind=kOutput, calls=%fused_computation.39 | convolution fusion | flops 1364852736 | bytes 9683072 | tf_op jit(solution)/shard_map/lip,rlbp->rlbi/dot_general | solution.py:225
  198.4 1.6 copy.43
  200.0 2.6 %reshape.210 = f32[96,16,384]{2,1,0:T(8,128)} reshape(f32[96,16,3,128]{3,2,1,0:T(4,128)S(1)} %copy.43) | data formatting | bytes 4718592 | tf_op jit(solution)/shard_map/reshape | solution.py:226
  (14 shorter events, 0.2 us)
Async XLA Ops:
  0.0 5.6 %copy-start.5 = (s32[4096]{0:T(1024)S(1)}, s32[4096]{0:T(1024)}, u32[]{:S(2)}) copy-start(s32[4096]{0:T(1024)} %param.11) | copy-start | bytes 49156
  0.0 5.6 %copy-start.4 = (f32[4096]{0:T(1024)S(1)}, f32[4096]{0:T(1024)}, u32[]{:S(2)}) copy-start(f32[4096]{0:T(1024)} %param.13) | copy-start | bytes 49156
  32.4 7.1 %copy-start.1 = (f32[385,16,97]{0,1,2:T(8,128)}, f32[385,16,97]{0,1,2:T(8,128)S(1)}, u32[]{:S(2)}) copy-start(f32[385,16,97]{0,1,2:T(8,128)S(1)} %copy.37) | copy-start | bytes 7170244
  32.4 6.9 %copy-start.6 = (f32[16]{0:T(128)S(1)}, f32[16]{0:T(128)}, u32[]{:S(2)}) copy-start(f32[16]{0:T(128)} %param.17) | copy-start | bytes 196
  32.4 6.9 %copy-start.7 = (f32[16]{0:T(128)S(1)}, f32[16]{0:T(128)}, u32[]{:S(2)}) copy-start(f32[16]{0:T(128)} %param.16) | copy-start | bytes 196
  35.5 7.1 %collective-permute-start = (f32[97,16]{0,1:T(8,128)S(1)}, f32[97,16]{0,1:T(8,128)S(1)}, u32[]{:S(2)}, u32[]{:S(2)}) collective-permute-start(f32[97,16]{0,1:T(8,128)S(1)} %bitcast.46), channel_id=1, source_target_pairs={{15,0},{0,1},{1,2},{2,3},{3,4},{4,5},{5,6},{6,7},{7,8},{8,9},{9,10... | collective-permute-start | bytes 18632 | tf_op jit(solution)/shard_map/ppermute | solution.py:16
  39.5 2.7 %copy-start.2 = (f32[97,16,1]{2,1,0:T(8,128)S(1)}, f32[97,16,1]{2,1,0:T(8,128)}, u32[]{:S(2)}) copy-start(f32[97,16,1]{2,1,0:T(8,128)} %get-tuple-element.11) | copy-start | bytes 18628
  43.1 7.4 %copy-start.3 = (f32[96,16,384]{2,1,0:T(8,128)S(1)}, f32[96,16,384]{2,1,0:T(8,128)}, u32[]{:S(2)}) copy-start(f32[96,16,384]{2,1,0:T(8,128)} %param.15) | copy-start | bytes 7077892
  43.1 7.3 %collective-permute-start.1 = (f32[16,384]{1,0:T(8,128)S(1)}, f32[16,384]{1,0:T(8,128)S(1)}, u32[]{:S(2)}, u32[]{:S(2)}) collective-permute-start(f32[16,384]{1,0:T(8,128)S(1)} %maximum_bitcast_fusion), channel_id=1, source_target_pairs={{0,16},{16,32},{32,48},{48,64},{64,80},{80,96},{96,112},{112,128},... | collective-permute-start | bytes 73736 | tf_op jit(solution)/shard_map/ppermute | solution.py:22
  152.1 3.5 %copy-start = (f32[96,16,384]{2,1,0:T(8,128)S(1)}, f32[96,16,384]{2,1,0:T(8,128)}, u32[]{:S(2)}) copy-start(f32[96,16,384]{2,1,0:T(8,128)} %fusion.27.x_ref) | copy-start | bytes 7077892
  162.4 27.7 %collective-permute-start.2 = (f32[96,16,128]{2,0,1:T(8,128)S(1)}, f32[96,16,128]{2,0,1:T(8,128)S(1)}, u32[]{:S(2)}, u32[]{:S(2)}) collective-permute-start(f32[96,16,128]{2,0,1:T(8,128)S(1)} %get-tuple-element.15), channel_id=1, source_target_pairs={{0,1},{1,2},{2,3},{3,4},{4,5},{5,6},{6,7},{7,8},{8,9},{9,10},{10,1... | collective-permute-start | bytes 2359304 | tf_op jit(solution)/shard_map/ppermute | solution.py:31
  181.2 13.3 %collective-permute-start.3 = (f32[96,16,128]{2,0,1:T(8,128)S(1)}, f32[96,16,128]{2,0,1:T(8,128)S(1)}, u32[]{:S(2)}, u32[]{:S(2)}) collective-permute-start(f32[96,16,128]{2,0,1:T(8,128)S(1)} %get-tuple-element.16), channel_id=1, source_target_pairs={{1,0},{2,1},{3,2},{4,3},{5,4},{6,5},{7,6},{8,7},{9,8},{10,9},{11,1... | collective-permute-start | bytes 2359304 | tf_op jit(solution)/shard_map/ppermute | solution.py:34

commit v6 on v5

--- a/solution.py
+++ b/solution.py
@@ -170,7 +170,7 @@
     halo_shape = jax.ShapeDtypeStruct((width,) + block.shape[1:], block.dtype)
     levels = block.shape[1]
     relay_shape = jax.ShapeDtypeStruct((4, rows, levels // 2, block.shape[2]), block.dtype)
-    pieces = 3 if rows % 3 == 0 else 1
+    pieces = 4 if rows % 4 == 0 else 1
     slots = 4 + 8 * pieces
     below, above, _ = pl.pallas_call(
         functools.partial(relay_halo_body, count, span, pieces, rows, far),

time: 203 us -> 204 us (level)
  no operation moved by 1% of the time
where the time goes in v6:
time: 204 us; the launch traced here: 203 us
  Pallas kernels  99.4 us (49%)
  matrix products  32.4 us (16%)
  starting transfers between devices  31.1 us (15%)
  local copies, waits for them, and re-layouts  15 us (7%)
  other arithmetic  11.9 us (6%)
  waiting for transfers between devices  11.9 us (6%)
    pallas_call x1, Pallas kernels, lat_halo_kernel(): pl.pallas_call(functools.partial(relay_halo_body, count, span, pieces, ro...  99.4 us
    dot_general x1, matrix products, shards(): jnp.einsum('klr,kc->rlc', row_values, col_w, precision=lax.Precision.HIGH)  22.9 us
    ppermute x1, starting transfers between devices, with_halo(): lax.ppermute(lax.slice_in_dim(block, block.shape[dim] - width, None, axis...  18.9 us
    ppermute x1, waiting for transfers between devices, with_halo(): lax.ppermute(lax.slice_in_dim(block, block.shape[dim] - width, None, axis...  6.59 us
    ppermute x1, starting transfers between devices, shifted(): return lax.ppermute(block, axis, route)  6.36 us
    dot_general x1, matrix products, shards(): jnp.einsum('lip,plc->ilc', lat_kernel, window, precision=lax.Precision.HIGH)  6.07 us
    ppermute x1, waiting for transfers between devices, with_halo(): lax.ppermute(lax.slice_in_dim(block, 0, width, axis=dim), axis, backward)  4.4 us
  transfers between devices with their start and end apart: 4, of which 3 were waited for; matrix products, arithmetic and copies ran while one was open for 2% of the time, Pallas kernels for 0%

profile of v6, /device:TPU:185, one launch (start us, length us, event | category | flops | bytes accessed | tf_op | source)
XLA Modules:
  0.0 202.8 jit_solution(6353469545231715207)
XLA Ops:
  0.0 0.0 copy-start.5
  0.0 0.0 copy-start.4
  0.0 0.7 broadcast_add_fusion
  0.7 0.7 broadcast_subtract_fusion
  2.1 0.7 broadcast_add_fusion.1
  2.8 0.7 broadcast_subtract_fusion.1
  3.6 1.0 select_add_fusion
  4.6 1.0 select_bitcast_fusion
  5.6 0.0 copy-done.5
  5.6 0.0 copy-done.4
  5.6 22.9 %fusion = f32[385,16,97]{2,0,1:T(8,128)} fusion(f32[4096,97]{0,1:T(8,128)S(1)} %select_add_fusion, f32[4096,16]{0,1:T(8,128)S(1)} %select_bitcast_fusion, f32[4096]{0:T(1024)S(1)} %copy-done.4, s32[4096]{0:T(1024)S(1)} %broadcast_add_fusion.1, f32[4096]{0:T(1024)S(1)} %broadcast_subtract_fusion.1, s32[4096]{0:T(1024)S(1)} %copy-done.5), kind=kOutput, calls=%fused_computation | convolution fusion | flops 14698893312 | bytes 4307008 | tf_op jit(solution)/shard_map/klr,kc->rlc/dot_general | solution.py:201
  28.5 3.9 %copy.37 = f32[385,16,97]{0,1,2:T(8,128)S(1)} copy(f32[385,16,97]{2,0,1:T(8,128)} %fusion) | data formatting | bytes 4780160 | tf_op jit(solution)/shard_map/klr,kc->rlc/dot_general | solution.py:201
  32.4 0.0 copy-start.1
  32.4 0.0 copy-start.6
  32.4 0.0 copy-start.7
  32.4 1.4 fusion.51
  33.8 1.6 copy.39
  35.5 3.7 %collective-permute-start = (f32[97,16]{0,1:T(8,128)S(1)}, f32[97,16]{0,1:T(8,128)S(1)}, u32[]{:S(2)}, u32[]{:S(2)}) collective-permute-start(f32[97,16]{0,1:T(8,128)S(1)} %bitcast.46), channel_id=1, source_target_pairs={{15,0},{0,1},{1,2},{2,3},{3,4},{4,5},{5,6},{6,7},{7,8},{8,9},{9,10... | collective-permute-start | bytes 18632 | tf_op jit(solution)/shard_map/ppermute | solution.py:16
  39.2 0.0 copy-done.6
  39.3 0.0 copy-done.7
  39.3 0.2 fusion.44
  39.5 0.0 copy-done.1
  39.5 0.0 copy-start.2
  39.5 2.6 %slice.44 = f32[97,16,383]{2,1,0:T(8,128)S(1)} slice(f32[97,16,385]{2,1,0:T(8,128)} %bitcast.42), slice={[0:97], [0:16], [1:384]} | slice | bytes 4755328 | tf_op jit(solution)/shard_map/slice | solution.py:206
  42.2 0.0 copy-done.2
  42.2 0.4 copy.38
  42.6 0.0 collective-permute-done
  42.6 0.5 copy.40
  43.0 0.1 maximum_bitcast_fusion
  43.1 0.0 copy-start.3
  43.1 6.4 %collective-permute-start.1 = (f32[16,384]{1,0:T(8,128)S(1)}, f32[16,384]{1,0:T(8,128)S(1)}, u32[]{:S(2)}, u32[]{:S(2)}) collective-permute-start(f32[16,384]{1,0:T(8,128)S(1)} %maximum_bitcast_fusion), channel_id=1, source_target_pairs={{0,16},{16,32},{32,48},{48,64},{64,80},{80,96},{96,112},{112,128},... | collective-permute-start | bytes 73736 | tf_op jit(solution)/shard_map/ppermute | solution.py:22
  49.5 0.9 collective-permute-done.1
  50.4 0.1 fusion.46
  50.5 0.0 copy-done.3
  50.5 2.2 %fusion.27.x_ref = f32[96,16,384]{2,1,0:T(8,128)} fusion(f32[96,16,384]{2,1,0:T(8,128)S(1)} %copy-done.3, f32[97,16,383]{2,1,0:T(8,128)S(1)} %slice.44, f32[97,16,1]{2,1,0:T(8,128)S(1)} %copy.40, f32[1,16,384]{2,1,0:T(8,128)S(1)} %fusion.46), kind=kLoop, calls=%fused_computation.34 | loop fusion | flops 3538944 | bytes 7127040 | tf_op jit(solution)/shard_map/mul | solution.py:210
  52.7 99.4 %shard_map.91 = (f32[128,16,384]{2,1,0:T(8,128)}, f32[128,16,384]{2,1,0:T(8,128)}, f32[4,96,8,384]{3,2,1,0:T(8,128)}) custom-call(f32[96,16,384]{2,1,0:T(8,128)} %fusion.27.x_ref), custom_call_target="tpu_custom_call" | custom-call | tf_op jit(solution)/shard_map/pallas_call | solution.py:175
  152.0 0.0 copy-start
  152.1 3.4 %broadcast_select_fusion = (f32[128,16,384]{2,1,0:T(8,128)S(1)}, f32[128,16,384]{2,1,0:T(8,128)S(1)}) fusion(f32[128,16,384]{2,1,0:T(8,128)} %get-tuple-element.8, pred[128]{0:T(512)(128)(4,1)S(1)} %compare_select_fusion, f32[128,16,384]{2,1,0:T(8,128)} %get-tuple-element.7, pred[128]{0:T(512)(128)(4,1)S(1)} %compare_select_fusion.1), kind=kLoop, calls=%fused_computation.44 | loop fusion | flops 1572864 | bytes 12583168 | tf_op jit(solution)/shard_map/jit(_where)/select_n | solution.py:186
  155.5 0.1 copy-done
  155.6 0.6 pad_maximum_fusion
  156.2 6.1 %fusion.4 = f32[16,384,96]{1,2,0:T(8,128)S(1)} fusion(f32[352,16,384]{2,1,0:T(8,128)S(1)} %pad_maximum_fusion, f32[16]{0:T(128)S(1)} %sqrt.14, f32[16]{0:T(128)S(1)} %get-tuple-element.19, f32[96,352]{1,0:T(8,128)S(1)} %multiply_negate_fusion.1, pred[96,352]{1,0:T(8,128)(4,1)S(1)} %abs_compare_fusion.1), kind=kOutput, calls=%fused_computation.5 | convolution fusion | flops 1247330304 | bytes 11179136 | tf_op jit(solution)/shard_map/lip,plc->ilc/dot_general | solution.py:214
  162.3 0.2 fusion.52
  162.4 18.9 %collective-permute-start.2 = (f32[96,16,128]{2,0,1:T(8,128)S(1)}, f32[96,16,128]{2,0,1:T(8,128)S(1)}, u32[]{:S(2)}, u32[]{:S(2)}) collective-permute-start(f32[96,16,128]{2,0,1:T(8,128)S(1)} %get-tuple-element.15), channel_id=1, source_target_pairs={{0,1},{1,2},{2,3},{3,4},{4,5},{5,6},{6,7},{7,8},{8,9},{9,10},{10,1... | collective-permute-start | bytes 2359304 | tf_op jit(solution)/shard_map/ppermute | solution.py:31
  181.4 2.2 %collective-permute-start.3 = (f32[96,16,128]{2,0,1:T(8,128)S(1)}, f32[96,16,128]{2,0,1:T(8,128)S(1)}, u32[]{:S(2)}, u32[]{:S(2)}) collective-permute-start(f32[96,16,128]{2,0,1:T(8,128)S(1)} %get-tuple-element.16), channel_id=1, source_target_pairs={{1,0},{2,1},{3,2},{4,3},{5,4},{6,5},{7,6},{8,7},{9,8},{10,9},{11,1... | collective-permute-start | bytes 2359304 | tf_op jit(solution)/shard_map/ppermute | solution.py:34
  183.6 0.1 abs_compare_fusion
  183.7 6.6 %collective-permute-done.2 = f32[96,16,128]{2,0,1:T(8,128)S(1)} collective-permute-done((f32[96,16,128]{2,0,1:T(8,128)S(1)}, f32[96,16,128]{2,0,1:T(8,128)S(1)}, u32[]{:S(2)}, u32[]{:S(2)}) %collective-permute-start.2) | collective-permute-done | bytes 786464 | tf_op jit(solution)/shard_map/ppermute | solution.py:31
  190.3 4.4 %collective-permute-done.3 = f32[96,16,128]{2,0,1:T(8,128)S(1)} collective-permute-done((f32[96,16,128]{2,0,1:T(8,128)S(1)}, f32[96,16,128]{2,0,1:T(8,128)S(1)}, u32[]{:S(2)}, u32[]{:S(2)}) %collective-permute-start.3) | collective-permute-done | bytes 786464 | tf_op jit(solution)/shard_map/ppermute | solution.py:34
  194.7 0.4 fusion.25
  195.0 3.5 %fusion.28 = f32[96,16,3,128]{3,0,2,1:T(8,128)S(1)} fusion(f32[16]{0:T(128)S(1)} %sqrt.15, f32[16]{0:T(128)S(1)} %get-tuple-element.17, f32[128,384]{1,0:T(8,128)S(1)} %multiply_negate_fusion, pred[128,384]{1,0:T(8,128)(4,1)S(1)} %abs_compare_fusion, f32[96,16,1,384]{3,0,1,2:T(8,128)S(1)} %get-tuple-element.14, f32[96,16,1,384]{3,0,1,2:T(8,128)S(1)} %bitcast.45, ...), kind=kOutput, calls=%fused_computation.39 | convolution fusion | flops 1364852736 | bytes 9683072 | tf_op jit(solution)/shard_map/lip,rlbp->rlbi/dot_general | solution.py:225
  198.5 1.6 copy.43
  200.2 2.6 %reshape.210 = f32[96,16,384]{2,1,0:T(8,128)} reshape(f32[96,16,3,128]{3,2,1,0:T(4,128)S(1)} %copy.43) | data formatting | bytes 4718592 | tf_op jit(solution)/shard_map/reshape | solution.py:226
  (14 shorter events, 0.2 us)
Async XLA Ops:
  0.0 5.6 %copy-start.5 = (s32[4096]{0:T(1024)S(1)}, s32[4096]{0:T(1024)}, u32[]{:S(2)}) copy-start(s32[4096]{0:T(1024)} %param.11) | copy-start | bytes 49156
  0.0 5.6 %copy-start.4 = (f32[4096]{0:T(1024)S(1)}, f32[4096]{0:T(1024)}, u32[]{:S(2)}) copy-start(f32[4096]{0:T(1024)} %param.13) | copy-start | bytes 49156
  32.4 7.1 %copy-start.1 = (f32[385,16,97]{0,1,2:T(8,128)}, f32[385,16,97]{0,1,2:T(8,128)S(1)}, u32[]{:S(2)}) copy-start(f32[385,16,97]{0,1,2:T(8,128)S(1)} %copy.37) | copy-start | bytes 7170244
  32.4 6.9 %copy-start.6 = (f32[16]{0:T(128)S(1)}, f32[16]{0:T(128)}, u32[]{:S(2)}) copy-start(f32[16]{0:T(128)} %param.17) | copy-start | bytes 196
  32.4 6.9 %copy-start.7 = (f32[16]{0:T(128)S(1)}, f32[16]{0:T(128)}, u32[]{:S(2)}) copy-start(f32[16]{0:T(128)} %param.16) | copy-start | bytes 196
  35.5 7.1 %collective-permute-start = (f32[97,16]{0,1:T(8,128)S(1)}, f32[97,16]{0,1:T(8,128)S(1)}, u32[]{:S(2)}, u32[]{:S(2)}) collective-permute-start(f32[97,16]{0,1:T(8,128)S(1)} %bitcast.46), channel_id=1, source_target_pairs={{15,0},{0,1},{1,2},{2,3},{3,4},{4,5},{5,6},{6,7},{7,8},{8,9},{9,10... | collective-permute-start | bytes 18632 | tf_op jit(solution)/shard_map/ppermute | solution.py:16
  39.5 2.7 %copy-start.2 = (f32[97,16,1]{2,1,0:T(8,128)S(1)}, f32[97,16,1]{2,1,0:T(8,128)}, u32[]{:S(2)}) copy-start(f32[97,16,1]{2,1,0:T(8,128)} %get-tuple-element.11) | copy-start | bytes 18628
  43.1 7.4 %copy-start.3 = (f32[96,16,384]{2,1,0:T(8,128)S(1)}, f32[96,16,384]{2,1,0:T(8,128)}, u32[]{:S(2)}) copy-start(f32[96,16,384]{2,1,0:T(8,128)} %param.15) | copy-start | bytes 7077892
  43.1 7.3 %collective-permute-start.1 = (f32[16,384]{1,0:T(8,128)S(1)}, f32[16,384]{1,0:T(8,128)S(1)}, u32[]{:S(2)}, u32[]{:S(2)}) collective-permute-start(f32[16,384]{1,0:T(8,128)S(1)} %maximum_bitcast_fusion), channel_id=1, source_target_pairs={{0,16},{16,32},{32,48},{48,64},{64,80},{80,96},{96,112},{112,128},... | collective-permute-start | bytes 73736 | tf_op jit(solution)/shard_map/ppermute | solution.py:22
  152.0 3.5 %copy-start = (f32[96,16,384]{2,1,0:T(8,128)S(1)}, f32[96,16,384]{2,1,0:T(8,128)}, u32[]{:S(2)}) copy-start(f32[96,16,384]{2,1,0:T(8,128)} %fusion.27.x_ref) | copy-start | bytes 7077892
  162.4 27.9 %collective-permute-start.2 = (f32[96,16,128]{2,0,1:T(8,128)S(1)}, f32[96,16,128]{2,0,1:T(8,128)S(1)}, u32[]{:S(2)}, u32[]{:S(2)}) collective-permute-start(f32[96,16,128]{2,0,1:T(8,128)S(1)} %get-tuple-element.15), channel_id=1, source_target_pairs={{0,1},{1,2},{2,3},{3,4},{4,5},{5,6},{6,7},{7,8},{8,9},{9,10},{10,1... | collective-permute-start | bytes 2359304 | tf_op jit(solution)/shard_map/ppermute | solution.py:31
  181.4 13.3 %collective-permute-start.3 = (f32[96,16,128]{2,0,1:T(8,128)S(1)}, f32[96,16,128]{2,0,1:T(8,128)S(1)}, u32[]{:S(2)}, u32[]{:S(2)}) collective-permute-start(f32[96,16,128]{2,0,1:T(8,128)S(1)} %get-tuple-element.16), channel_id=1, source_target_pairs={{1,0},{2,1},{3,2},{4,3},{5,4},{6,5},{7,6},{8,7},{9,8},{10,9},{11,1... | collective-permute-start | bytes 2359304 | tf_op jit(solution)/shard_map/ppermute | solution.py:34

commit v7 on v5

--- a/solution.py
+++ b/solution.py
@@ -94,8 +94,10 @@
     near_below = below_ref.at[pl.ds(far, rows)]
     near_above = above_ref.at[pl.ds(0, rows)]
     plan = [
-        (here + 2 < count, 2, x_ref.at[pl.ds(rows - far, far)], below_ref.at[pl.ds(0, far)], here >= 2),
-        (here >= 2, -2, x_ref.at[pl.ds(0, far)], above_ref.at[pl.ds(rows, far)], here + 2 < count),
+        (jnp.logical_and(here + 2 < count, here % span < span - 2), 2, x_ref.at[pl.ds(rows - far, far)],
+         below_ref.at[pl.ds(0, far)], jnp.logical_and(here >= 2, here % span >= 2)),
+        (jnp.logical_and(here >= 2, here % span >= 2), -2, x_ref.at[pl.ds(0, far)],
+         above_ref.at[pl.ds(rows, far)], jnp.logical_and(here + 2 < count, here % span < span - 2)),
         (jnp.logical_and(up_exists, jnp.logical_not(cross_up)), 1, x_ref, near_below,
          jnp.logical_and(down_exists, jnp.logical_not(first_of))),
         (jnp.logical_and(down_exists, jnp.logical_not(first_of)), -1, x_ref, near_above,
@@ -118,6 +120,29 @@
             plan.append((start, first_hop, x_ref.at[part, levels], relay_ref.at[slot, part], relays))
             feeds[len(plan)] = len(plan) - 1
             plan.append((relays, second_hop, relay_ref.at[slot, part], target.at[part, levels], lands))
+    top_rows = x_ref.at[pl.ds(rows - far, far)]
+    bottom_rows = x_ref.at[pl.ds(0, far)]
+    edge = pl.ds(0, far)
+    for lane in (span - 2, span - 1):
+        up_start = jnp.logical_and(here % span == lane, here + 2 < count)
+        up_a = jnp.logical_and(here % span == lane, here >= span)
+        up_b = jnp.logical_and(here % span == lane + 2 - span, here + span < count)
+        up_lands = jnp.logical_and(here % span == lane + 2 - span, here >= span)
+        down_start = jnp.logical_and(here % span == lane + 2 - span, here >= span)
+        down_lands = jnp.logical_and(here % span == lane, here + 2 < count)
+        far_routes = [
+            (up_start, span, top_rows.at[:, low], 4, up_a, 2 - span, below_ref.at[edge, low], up_lands),
+            (up_start, 2 - span, top_rows.at[:, high], 5, up_b, span, below_ref.at[edge, high], up_lands),
+            (down_start, -span, bottom_rows.at[:, low], 6, up_b, span - 2,
+             above_ref.at[pl.ds(rows, far), low], down_lands),
+            (down_start, span - 2, bottom_rows.at[:, high], 7, up_a, -span,
+             above_ref.at[pl.ds(rows, far), high], down_lands),
+        ]
+        for start, first_hop, source, slot, relays, second_hop, target, lands in far_routes:
+            held = relay_ref.at[slot, pl.ds((lane - span + 2) * far, far)]
+            plan.append((start, first_hop, source, held, relays))
+            feeds[len(plan)] = len(plan) - 1
+            plan.append((relays, second_hop, held, target, lands))
 
     barrier = pltpu.get_barrier_semaphore()
     offsets = sorted({entry[1] for entry in plan})
@@ -169,9 +194,9 @@
     count = lax.axis_size("lat")
     halo_shape = jax.ShapeDtypeStruct((width,) + block.shape[1:], block.dtype)
     levels = block.shape[1]
-    relay_shape = jax.ShapeDtypeStruct((4, rows, levels // 2, block.shape[2]), block.dtype)
+    relay_shape = jax.ShapeDtypeStruct((8, rows, levels // 2, block.shape[2]), block.dtype)
     pieces = 3 if rows % 3 == 0 else 1
-    slots = 4 + 8 * pieces
+    slots = 4 + 8 * pieces + 16
     below, above, _ = pl.pallas_call(
         functools.partial(relay_halo_body, count, span, pieces, rows, far),
         out_shape=(halo_shape, halo_shape, relay_shape),

time: 203 us -> 204 us (level)
  the two profiles are of different devices: /device:TPU:185 before, /device:TPU:57 now
where the time goes in v7:
time: 204 us; the launch traced here: 203 us
  Pallas kernels  116 us (57%)
  matrix products  32.4 us (16%)
  local copies, waits for them, and re-layouts  15 us (7%)
  starting transfers between devices  14.5 us (7%)
  other arithmetic  11.9 us (6%)
  waiting for transfers between devices  11.9 us (6%)
    pallas_call x1, Pallas kernels, lat_halo_kernel(): pl.pallas_call(functools.partial(relay_halo_body, count, span, pieces, ro...  116 us
    dot_general x1, matrix products, shards(): jnp.einsum('klr,kc->rlc', row_values, col_w, precision=lax.Precision.HIGH)  22.9 us
    ppermute x1, waiting for transfers between devices, with_halo(): lax.ppermute(lax.slice_in_dim(block, block.shape[dim] - width, None, axis...  6.59 us
    dot_general x1, matrix products, shards(): jnp.einsum('lip,plc->ilc', lat_kernel, window, precision=lax.Precision.HIGH)  6.07 us
    ppermute x1, starting transfers between devices, shifted(): return lax.ppermute(block, axis, route)  5.14 us
    ppermute x1, waiting for transfers between devices, with_halo(): lax.ppermute(lax.slice_in_dim(block, 0, width, axis=dim), axis, backward)  4.4 us
  transfers between devices with their start and end apart: 4, of which 3 were waited for; matrix products, arithmetic and copies ran while one was open for 2% of the time, Pallas kernels for 0%

profile of v7, /device:TPU:57, one launch (start us, length us, event | category | flops | bytes accessed | tf_op | source)
XLA Modules:
  0.0 203.2 jit_solution(16737117727602784743)
XLA Ops:
  0.0 0.0 copy-start.5
  0.0 0.0 copy-start.4
  0.0 0.7 broadcast_add_fusion
  0.7 0.7 broadcast_subtract_fusion
  2.1 0.7 broadcast_add_fusion.1
  2.8 0.7 broadcast_subtract_fusion.1
  3.6 1.0 select_add_fusion
  4.6 1.0 select_bitcast_fusion
  5.6 0.0 copy-done.5
  5.6 0.0 copy-done.4
  5.6 22.9 %fusion = f32[385,16,97]{2,0,1:T(8,128)} fusion(f32[4096,97]{0,1:T(8,128)S(1)} %select_add_fusion, f32[4096,16]{0,1:T(8,128)S(1)} %select_bitcast_fusion, f32[4096]{0:T(1024)S(1)} %copy-done.4, s32[4096]{0:T(1024)S(1)} %broadcast_add_fusion.1, f32[4096]{0:T(1024)S(1)} %broadcast_subtract_fusion.1, s32[4096]{0:T(1024)S(1)} %copy-done.5), kind=kOutput, calls=%fused_computation | convolution fusion | flops 14698893312 | bytes 4307008 | tf_op jit(solution)/shard_map/klr,kc->rlc/dot_general | solution.py:226
  28.5 3.9 %copy.37 = f32[385,16,97]{0,1,2:T(8,128)S(1)} copy(f32[385,16,97]{2,0,1:T(8,128)} %fusion) | data formatting | bytes 4780160 | tf_op jit(solution)/shard_map/klr,kc->rlc/dot_general | solution.py:226
  32.4 0.0 copy-start.1
  32.4 0.0 copy-start.6
  32.4 0.0 copy-start.7
  32.4 1.4 fusion.51
  33.8 1.6 copy.39
  35.5 3.7 %collective-permute-start = (f32[97,16]{0,1:T(8,128)S(1)}, f32[97,16]{0,1:T(8,128)S(1)}, u32[]{:S(2)}, u32[]{:S(2)}) collective-permute-start(f32[97,16]{0,1:T(8,128)S(1)} %bitcast.46), channel_id=1, source_target_pairs={{15,0},{0,1},{1,2},{2,3},{3,4},{4,5},{5,6},{6,7},{7,8},{8,9},{9,10... | collective-permute-start | bytes 18632 | tf_op jit(solution)/shard_map/ppermute | solution.py:16
  39.2 0.0 copy-done.6
  39.3 0.0 copy-done.7
  39.3 0.2 fusion.44
  39.5 0.0 copy-done.1
  39.5 0.0 copy-start.2
  39.5 2.6 %slice.44 = f32[97,16,383]{2,1,0:T(8,128)S(1)} slice(f32[97,16,385]{2,1,0:T(8,128)} %bitcast.42), slice={[0:97], [0:16], [1:384]} | slice | bytes 4755328 | tf_op jit(solution)/shard_map/slice | solution.py:231
  42.2 0.0 copy-done.2
  42.2 0.4 copy.38
  42.6 0.0 collective-permute-done
  42.6 0.5 copy.40
  43.0 0.1 maximum_bitcast_fusion
  43.1 0.0 copy-start.3
  43.1 5.1 %collective-permute-start.1 = (f32[16,384]{1,0:T(8,128)S(1)}, f32[16,384]{1,0:T(8,128)S(1)}, u32[]{:S(2)}, u32[]{:S(2)}) collective-permute-start(f32[16,384]{1,0:T(8,128)S(1)} %maximum_bitcast_fusion), channel_id=1, source_target_pairs={{0,16},{16,32},{32,48},{48,64},{64,80},{80,96},{96,112},{112,128},... | collective-permute-start | bytes 73736 | tf_op jit(solution)/shard_map/ppermute | solution.py:22
  48.3 0.9 collective-permute-done.1
  49.2 0.1 fusion.46
  49.3 0.0 copy-done.3
  49.3 2.2 %fusion.27.x_ref = f32[96,16,384]{2,1,0:T(8,128)} fusion(f32[96,16,384]{2,1,0:T(8,128)S(1)} %copy-done.3, f32[97,16,383]{2,1,0:T(8,128)S(1)} %slice.44, f32[97,16,1]{2,1,0:T(8,128)S(1)} %copy.40, f32[1,16,384]{2,1,0:T(8,128)S(1)} %fusion.46), kind=kLoop, calls=%fused_computation.34 | loop fusion | flops 3538944 | bytes 7127040 | tf_op jit(solution)/shard_map/mul | solution.py:235
  51.4 116.4 %shard_map.91 = (f32[128,16,384]{2,1,0:T(8,128)}, f32[128,16,384]{2,1,0:T(8,128)}, f32[8,96,8,384]{3,2,1,0:T(8,128)}) custom-call(f32[96,16,384]{2,1,0:T(8,128)} %fusion.27.x_ref), custom_call_target="tpu_custom_call" | custom-call | tf_op jit(solution)/shard_map/pallas_call | solution.py:200
  167.9 0.0 copy-start
  167.9 3.4 %broadcast_select_fusion = (f32[128,16,384]{2,1,0:T(8,128)S(1)}, f32[128,16,384]{2,1,0:T(8,128)S(1)}) fusion(f32[128,16,384]{2,1,0:T(8,128)} %get-tuple-element.8, pred[128]{0:T(512)(128)(4,1)S(1)} %compare_select_fusion, f32[128,16,384]{2,1,0:T(8,128)} %get-tuple-element.7, pred[128]{0:T(512)(128)(4,1)S(1)} %compare_select_fusion.1), kind=kLoop, calls=%fused_computation.44 | loop fusion | flops 1572864 | bytes 12583168 | tf_op jit(solution)/shard_map/jit(_where)/select_n | solution.py:211
  171.3 0.1 copy-done
  171.4 0.6 pad_maximum_fusion
  172.0 6.1 %fusion.4 = f32[16,384,96]{1,2,0:T(8,128)S(1)} fusion(f32[352,16,384]{2,1,0:T(8,128)S(1)} %pad_maximum_fusion, f32[16]{0:T(128)S(1)} %sqrt.14, f32[16]{0:T(128)S(1)} %get-tuple-element.19, f32[96,352]{1,0:T(8,128)S(1)} %multiply_negate_fusion.1, pred[96,352]{1,0:T(8,128)(4,1)S(1)} %abs_compare_fusion.1), kind=kOutput, calls=%fused_computation.5 | convolution fusion | flops 1247330304 | bytes 11179136 | tf_op jit(solution)/shard_map/lip,plc->ilc/dot_general | solution.py:239
  178.1 0.2 fusion.52
  178.3 3.5 %collective-permute-start.2 = (f32[96,16,128]{2,0,1:T(8,128)S(1)}, f32[96,16,128]{2,0,1:T(8,128)S(1)}, u32[]{:S(2)}, u32[]{:S(2)}) collective-permute-start(f32[96,16,128]{2,0,1:T(8,128)S(1)} %get-tuple-element.15), channel_id=1, source_target_pairs={{0,1},{1,2},{2,3},{3,4},{4,5},{5,6},{6,7},{7,8},{8,9},{9,10},{10,1... | collective-permute-start | bytes 2359304 | tf_op jit(solution)/shard_map/ppermute | solution.py:31
  181.8 2.2 %collective-permute-start.3 = (f32[96,16,128]{2,0,1:T(8,128)S(1)}, f32[96,16,128]{2,0,1:T(8,128)S(1)}, u32[]{:S(2)}, u32[]{:S(2)}) collective-permute-start(f32[96,16,128]{2,0,1:T(8,128)S(1)} %get-tuple-element.16), channel_id=1, source_target_pairs={{1,0},{2,1},{3,2},{4,3},{5,4},{6,5},{7,6},{8,7},{9,8},{10,9},{11,1... | collective-permute-start | bytes 2359304 | tf_op jit(solution)/shard_map/ppermute | solution.py:34
  184.0 0.1 abs_compare_fusion
  184.1 6.6 %collective-permute-done.2 = f32[96,16,128]{2,0,1:T(8,128)S(1)} collective-permute-done((f32[96,16,128]{2,0,1:T(8,128)S(1)}, f32[96,16,128]{2,0,1:T(8,128)S(1)}, u32[]{:S(2)}, u32[]{:S(2)}) %collective-permute-start.2) | collective-permute-done | bytes 786464 | tf_op jit(solution)/shard_map/ppermute | solution.py:31
  190.7 4.4 %collective-permute-done.3 = f32[96,16,128]{2,0,1:T(8,128)S(1)} collective-permute-done((f32[96,16,128]{2,0,1:T(8,128)S(1)}, f32[96,16,128]{2,0,1:T(8,128)S(1)}, u32[]{:S(2)}, u32[]{:S(2)}) %collective-permute-start.3) | collective-permute-done | bytes 786464 | tf_op jit(solution)/shard_map/ppermute | solution.py:34
  195.1 0.4 fusion.25
  195.4 3.5 %fusion.28 = f32[96,16,3,128]{3,0,2,1:T(8,128)S(1)} fusion(f32[16]{0:T(128)S(1)} %sqrt.15, f32[16]{0:T(128)S(1)} %get-tuple-element.17, f32[128,384]{1,0:T(8,128)S(1)} %multiply_negate_fusion, pred[128,384]{1,0:T(8,128)(4,1)S(1)} %abs_compare_fusion, f32[96,16,1,384]{3,0,1,2:T(8,128)S(1)} %get-tuple-element.14, f32[96,16,1,384]{3,0,1,2:T(8,128)S(1)} %bitcast.45, ...), kind=kOutput, calls=%fused_computation.39 | convolution fusion | flops 1364852736 | bytes 9683072 | tf_op jit(solution)/shard_map/lip,rlbp->rlbi/dot_general | solution.py:250
  198.9 1.6 copy.43
  200.6 2.6 %reshape.210 = f32[96,16,384]{2,1,0:T(8,128)} reshape(f32[96,16,3,128]{3,2,1,0:T(4,128)S(1)} %copy.43) | data formatting | bytes 4718592 | tf_op jit(solution)/shard_map/reshape | solution.py:251
  (14 shorter events, 0.2 us)
Async XLA Ops:
  0.0 5.6 %copy-start.5 = (s32[4096]{0:T(1024)S(1)}, s32[4096]{0:T(1024)}, u32[]{:S(2)}) copy-start(s32[4096]{0:T(1024)} %param.11) | copy-start | bytes 49156
  0.0 5.6 %copy-start.4 = (f32[4096]{0:T(1024)S(1)}, f32[4096]{0:T(1024)}, u32[]{:S(2)}) copy-start(f32[4096]{0:T(1024)} %param.13) | copy-start | bytes 49156
  32.4 7.1 %copy-start.1 = (f32[385,16,97]{0,1,2:T(8,128)}, f32[385,16,97]{0,1,2:T(8,128)S(1)}, u32[]{:S(2)}) copy-start(f32[385,16,97]{0,1,2:T(8,128)S(1)} %copy.37) | copy-start | bytes 7170244
  32.4 6.9 %copy-start.6 = (f32[16]{0:T(128)S(1)}, f32[16]{0:T(128)}, u32[]{:S(2)}) copy-start(f32[16]{0:T(128)} %param.17) | copy-start | bytes 196
  32.4 6.9 %copy-start.7 = (f32[16]{0:T(128)S(1)}, f32[16]{0:T(128)}, u32[]{:S(2)}) copy-start(f32[16]{0:T(128)} %param.16) | copy-start | bytes 196
  35.5 7.1 %collective-permute-start = (f32[97,16]{0,1:T(8,128)S(1)}, f32[97,16]{0,1:T(8,128)S(1)}, u32[]{:S(2)}, u32[]{:S(2)}) collective-permute-start(f32[97,16]{0,1:T(8,128)S(1)} %bitcast.46), channel_id=1, source_target_pairs={{15,0},{0,1},{1,2},{2,3},{3,4},{4,5},{5,6},{6,7},{7,8},{8,9},{9,10... | collective-permute-start | bytes 18632 | tf_op jit(solution)/shard_map/ppermute | solution.py:16
  39.5 2.7 %copy-start.2 = (f32[97,16,1]{2,1,0:T(8,128)S(1)}, f32[97,16,1]{2,1,0:T(8,128)}, u32[]{:S(2)}) copy-start(f32[97,16,1]{2,1,0:T(8,128)} %get-tuple-element.11) | copy-start | bytes 18628
  43.1 6.2 %copy-start.3 = (f32[96,16,384]{2,1,0:T(8,128)S(1)}, f32[96,16,384]{2,1,0:T(8,128)}, u32[]{:S(2)}) copy-start(f32[96,16,384]{2,1,0:T(8,128)} %param.15) | copy-start | bytes 7077892
  43.1 6.1 %collective-permute-start.1 = (f32[16,384]{1,0:T(8,128)S(1)}, f32[16,384]{1,0:T(8,128)S(1)}, u32[]{:S(2)}, u32[]{:S(2)}) collective-permute-start(f32[16,384]{1,0:T(8,128)S(1)} %maximum_bitcast_fusion), channel_id=1, source_target_pairs={{0,16},{16,32},{32,48},{48,64},{64,80},{80,96},{96,112},{112,128},... | collective-permute-start | bytes 73736 | tf_op jit(solution)/shard_map/ppermute | solution.py:22
  167.9 3.5 %copy-start = (f32[96,16,384]{2,1,0:T(8,128)S(1)}, f32[96,16,384]{2,1,0:T(8,128)}, u32[]{:S(2)}) copy-start(f32[96,16,384]{2,1,0:T(8,128)} %fusion.27.x_ref) | copy-start | bytes 7077892
  178.3 12.4 %collective-permute-start.2 = (f32[96,16,128]{2,0,1:T(8,128)S(1)}, f32[96,16,128]{2,0,1:T(8,128)S(1)}, u32[]{:S(2)}, u32[]{:S(2)}) collective-permute-start(f32[96,16,128]{2,0,1:T(8,128)S(1)} %get-tuple-element.15), channel_id=1, source_target_pairs={{0,1},{1,2},{2,3},{3,4},{4,5},{5,6},{6,7},{7,8},{8,9},{9,10},{10,1... | collective-permute-start | bytes 2359304 | tf_op jit(solution)/shard_map/ppermute | solution.py:31
  181.8 13.3 %collective-permute-start.3 = (f32[96,16,128]{2,0,1:T(8,128)S(1)}, f32[96,16,128]{2,0,1:T(8,128)S(1)}, u32[]{:S(2)}, u32[]{:S(2)}) collective-permute-start(f32[96,16,128]{2,0,1:T(8,128)S(1)} %get-tuple-element.16), channel_id=1, source_target_pairs={{1,0},{2,1},{3,2},{4,3},{5,4},{6,5},{7,6},{8,7},{9,8},{10,9},{11,1... | collective-permute-start | bytes 2359304 | tf_op jit(solution)/shard_map/ppermute | solution.py:34
